TPU v7x, 32 devices: a whole 2x2x4 slice. The times are simulated.
32 devices in a mesh: expert: 8 (over z, y), shard: 4 (over x, core).
Axes of the slice: x: 2, y: 2, z: 4, core: 2. Of those that a mesh axis runs over, the one named last changes fastest.
Arguments:
- hidden: bfloat16 [8, 512, 2048], P('expert', 'shard'), may hold values from -12 to 12
- cotangent: bfloat16 [8, 512, 2048], P('expert', 'shard'), may hold values from -6 to 6
- segments: int32 [8, 512], P('expert'), may hold values from 0 to 3, as said below
- routes: int32 [8, 512, 6], P('expert', 'shard'), may hold values from 0 to 31, all different within a row; in each aligned block of 128 rows (0 to 127, 128 to 255, ..., all dimensions but the last counted through in order) at most 32 rows name the same one
- w_query: bfloat16 [2048, 3072], P('shard'), may hold values from -0.125 to 0.125
- w_latent: bfloat16 [2048, 576], P('shard'), may hold values from -0.125 to 0.125
- g_latent: bfloat16 [512], P('shard'), may hold values from 0.099609375 to 1.8984375
- w_expand: bfloat16 [512, 4096], P('shard'), may hold values from -0.25 to 0.25
- w_out: bfloat16 [2048, 2048], P('shard'), may hold values from -1 to 1
- g_attn: bfloat16 [2048], P('shard'), may hold values from 0.099609375 to 1.8984375
- g_ffn: bfloat16 [2048], P('shard'), may hold values from 0.099609375 to 1.8984375
- w_router: bfloat16 [2048, 32], P('shard'), may hold values from -0.125 to 0.125
- s_gate: bfloat16 [2048, 2816], P('shard'), may hold values from -0.125 to 0.125
- s_up: bfloat16 [2048, 2816], P('shard'), may hold values from -0.125 to 0.125
- s_down: bfloat16 [2816, 2048], P('shard'), may hold values from -0.109375 to 0.109375
- e_gate: bfloat16 [32, 2048, 1408], P('expert', None, 'shard'), may hold values from -0.125 to 0.125
- expert_up_weight: bfloat16 [32, 2048, 1408], P('expert', None, 'shard'), may hold values from -0.125 to 0.125
- e_down: bfloat16 [32, 1408, 2048], P('expert', 'shard'), may hold values from -0.15625 to 0.15625
Outputs:
- output: bfloat16 [8, 512, 2048], P('expert', 'shard')
- d_hidden: float32 [8, 512, 2048], P('expert', 'shard')
- d_query: float32 [2048, 3072], P('shard')
- d_latent: float32 [2048, 576], P('shard')
- d_glatent: float32 [512], P('shard')
- d_expand: float32 [512, 4096], P('shard')
- d_out: float32 [2048, 2048], P('shard')
- d_gattn: float32 [2048], P('shard')
- d_gffn: float32 [2048], P('shard')
- d_router: float32 [2048, 32], P('shard')
- d_sgate: float32 [2048, 2816], P('shard')
- d_sup: float32 [2048, 2816], P('shard')
- d_sdown: float32 [2816, 2048], P('shard')
- d_egate: float32 [32, 2048, 1408], P('expert', None, 'shard')
- grad_expert_up: float32 [32, 2048, 1408], P('expert', None, 'shard')
- d_edown: float32 [32, 1408, 2048], P('expert', 'shard')
Inputs may be any that keep to these rules, and one draw needn't show every extreme that they name: `segments`: along each sequence the ids start at 0 and rise by one at each document boundary; each sequence holds 2 to 4 documents of 102 positions or more, and some sequence holds 4. `routes`: each token names 6 different experts; among the rows of one device no expert is named by more than 32 of them, a bound that some block reaches of one device.
All inputs are finite; a program needn't handle non-finite values.
Results may differ from a plain program's by a relative error of at most 0.019.
Values may be sent and summed in bfloat16 or wider, within the bound.
No kernel may reach another device: no remote copies, remote signals or barrier semaphores. Data moves between devices by JAX's collectives and lax.ppermute only.
A program may use at most 640 MiB of HBM per device.

v0:
```python
import jax
import jax.numpy as jnp
from jax import lax
from jax.sharding import PartitionSpec as P

H = 16
DN = 128
DR = 64
DV = 128
KVR = 512
TOP = 6
EXP_DEV = 4


EPS = 1e-06
ROUTE_SCALE = 2.446
ROPE_BASE = 50000.0


def matmul(first_op, second_op):
    return jnp.dot(first_op, second_op, preferred_element_type=jnp.float32)


def inner_rows(first_op, second_op):
    return lax.dot_general(
        first_op, second_op, (((0,), (0,)), ((), ())), preferred_element_type=jnp.float32
    )


def outer_cols(first_op, second_op):
    return lax.dot_general(
        first_op, second_op, (((1,), (1,)), ((), ())), preferred_element_type=jnp.float32
    )


def rope_angles(positions):
    half_width = DR // 2
    inverse = ROPE_BASE ** (-jnp.arange(half_width).astype(jnp.float32) / half_width)
    angles = positions.astype(jnp.float32)[:, None] * inverse[None, :]
    return (jnp.cos(angles), jnp.sin(angles))


def rotate(values, cosine, sine_vals):
    half_width = values.shape[-1] // 2
    first_half = values[..., :half_width]
    second_half = values[..., half_width:]
    return jnp.concatenate(
        [
            first_half * cosine - second_half * sine_vals,
            second_half * cosine + first_half * sine_vals,
        ],
        axis=-1,
    )


def norm_forward(values, gain_vec):
    factor = lax.rsqrt(jnp.mean(values * values, axis=-1, keepdims=True) + EPS)
    unit_vals = values * factor
    return (unit_vals * gain_vec, unit_vals, factor)


def norm_backward(grad_out, gain_vec, unit_vals, factor):
    grad_unit = grad_out * gain_vec
    grad_in = factor * (
        grad_unit - unit_vals * jnp.mean(grad_unit * unit_vals, axis=-1, keepdims=True)
    )
    return (grad_in, jnp.sum(grad_out * unit_vals, axis=0))


def swish_gradients(gate_preactivation, up_preactivation, grad_inner_hidden):
    sigmoid_g = jax.nn.sigmoid(gate_preactivation)
    grad_gate = (
        grad_inner_hidden
        * up_preactivation
        * sigmoid_g
        * (1.0 + gate_preactivation * (1.0 - sigmoid_g))
    )
    grad_up = grad_inner_hidden * (gate_preactivation * sigmoid_g)
    return (grad_gate.astype(jnp.bfloat16), grad_up.astype(jnp.bfloat16))


def route_ranks(route_block, experts):
    flat_routes = route_block.reshape(-1)
    hit_table = (flat_routes[:, None] == jnp.arange(experts, dtype=jnp.int32)[None, :]).astype(
        jnp.int32
    )
    before = jnp.cumsum(hit_table, axis=0) - hit_table
    return jnp.sum(before * hit_table, axis=1)


def spread_copies(rows_in, groups, shards):
    block_rows = rows_in.shape[0] // groups
    shaped = rows_in.reshape(groups, 1, block_rows, rows_in.shape[1])
    return jnp.broadcast_to(shaped, (groups, shards, block_rows, rows_in.shape[1])).reshape(
        groups * shards * block_rows, rows_in.shape[1]
    )


def fold_slices(rows_in, groups, shards):
    block_rows = rows_in.shape[0] // (groups * shards)
    return jnp.sum(rows_in.reshape(groups, shards, block_rows, rows_in.shape[1]), axis=1).reshape(
        groups * block_rows, rows_in.shape[1]
    )


def column_pieces(values, shards):
    return values.reshape(values.shape[0], shards, values.shape[1] // shards)


def full_copies(values, shards):
    return jnp.broadcast_to(values[:, None, :], (values.shape[0], shards, values.shape[1]))


def body(
    hidden,
    cotangent,
    segments,
    routes,
    w_query,
    w_latent,
    g_latent,
    w_expand,
    w_out,
    g_attn,
    g_ffn,
    w_router,
    s_gate,
    s_up,
    s_down,
    e_gate,
    expert_up_weight,
    e_down,
):
    tokens_here = hidden.shape[1]
    width = hidden.shape[2]
    shards = lax.axis_size("shard")
    groups = lax.axis_size("expert")
    devices = lax.axis_size(("expert", "shard"))
    experts = EXP_DEV * groups
    capacity = max(2, tokens_here * TOP * 4 // (3 * experts))
    (
        full_query,
        full_latent,
        full_glatent,
        full_expand,
        full_out,
        full_gattn,
        full_gffn,
        full_router,
        full_sgate,
        full_sup,
        full_sdown,
    ) = (
        lax.all_gather(w_query, "shard", axis=0, tiled=True),
        lax.all_gather(w_latent, "shard", axis=0, tiled=True),
        lax.all_gather(g_latent, "shard", axis=0, tiled=True),
        lax.all_gather(w_expand, "shard", axis=0, tiled=True),
        lax.all_gather(w_out, "shard", axis=0, tiled=True),
        lax.all_gather(g_attn, "shard", axis=0, tiled=True),
        lax.all_gather(g_ffn, "shard", axis=0, tiled=True),
        lax.all_gather(w_router, "shard", axis=0, tiled=True),
        lax.all_gather(s_gate, "shard", axis=0, tiled=True),
        lax.all_gather(s_up, "shard", axis=0, tiled=True),
        lax.all_gather(s_down, "shard", axis=0, tiled=True),
    )
    residual_in = hidden[0].astype(jnp.float32)
    first_norm_gain = full_gattn.astype(jnp.float32)
    normed_f, unit_one, factor_one = norm_forward(residual_in, first_norm_gain)
    normed = normed_f.astype(jnp.bfloat16)
    offset = lax.axis_index("shard") * tokens_here
    local_pos = offset + jnp.arange(tokens_here, dtype=jnp.int32)
    cos_local, sin_local = rope_angles(local_pos)
    query_pre = matmul(normed, full_query).reshape(tokens_here, H, DN + DR)
    query_in = jnp.concatenate(
        [
            query_pre[..., :DN],
            rotate(query_pre[..., DN:], cos_local[:, None, :], sin_local[:, None, :]),
        ],
        axis=-1,
    ).astype(jnp.bfloat16)
    compressed = matmul(normed, full_latent)
    glatent = full_glatent.astype(jnp.float32)
    latent_norm, latent_unit, latent_factor = norm_forward(compressed[:, :KVR], glatent)
    latent_local = jnp.concatenate(
        [latent_norm, rotate(compressed[:, KVR:], cos_local, sin_local)], axis=1
    ).astype(jnp.bfloat16)
    latent_all = lax.all_gather(latent_local, "shard", axis=0, tiled=True)
    key_count = latent_all.shape[0]
    expanded = (
        matmul(latent_all[:, :KVR], full_expand).astype(jnp.bfloat16).reshape(key_count, H, DN + DV)
    )
    key_nope = expanded[..., :DN]
    values_all = expanded[..., DN:]
    key_rope = latent_all[:, KVR:]
    seg_row = segments[0]
    seg_local = lax.dynamic_slice_in_dim(seg_row, offset, tokens_here, 0)
    key_pos = jnp.arange(key_count, dtype=jnp.int32)
    allowed = (seg_local[:, None] == seg_row[None, :]) & (key_pos[None, :] <= local_pos[:, None])
    score_scale = (DN + DR) ** (-0.5)

    def masked_scores():
        raw_scores = jnp.einsum(
            "qhd,khd->hqk", query_in[..., :DN], key_nope, preferred_element_type=jnp.float32
        ) + jnp.einsum(
            "qhd,kd->hqk", query_in[..., DN:], key_rope, preferred_element_type=jnp.float32
        )
        return jnp.where(allowed[None], raw_scores * score_scale, -1e30)

    scores = masked_scores()
    top_score = jnp.max(scores, axis=-1, keepdims=True)
    exponent = jnp.exp(scores - top_score)
    row_total = jnp.sum(exponent, axis=-1, keepdims=True)
    log_total = top_score + jnp.log(row_total)
    weights_b = (exponent / row_total).astype(jnp.bfloat16)
    attended = (
        jnp.einsum("hqk,khd->qhd", weights_b, values_all, preferred_element_type=jnp.float32)
        .astype(jnp.bfloat16)
        .reshape(tokens_here, H * DV)
    )
    attn_out = matmul(attended, full_out)
    residual_mid = residual_in + attn_out
    second_norm_gain = full_gffn.astype(jnp.float32)
    normed_two_f, unit_two, factor_two = norm_forward(residual_mid, second_norm_gain)
    normed_two = normed_two_f.astype(jnp.bfloat16)
    logits = matmul(normed_two, full_router)
    probs_r = jax.nn.sigmoid(logits)
    local_routes = routes[0]
    choose = local_routes[:, :, None] == jnp.arange(experts, dtype=jnp.int32)[None, None, :]
    chosen = jnp.sum(jnp.where(choose, probs_r[:, None, :], 0.0), axis=-1)
    chosen_total = jnp.sum(chosen, axis=1, keepdims=True)
    route_weights = chosen / chosen_total * ROUTE_SCALE
    slot_rank = route_ranks(local_routes, experts)
    slot_of = local_routes.reshape(-1) * capacity + slot_rank
    pair_count = tokens_here * TOP
    pair_of_slot = (
        jnp.full((experts * capacity,), pair_count, jnp.int32)
        .at[slot_of]
        .set(jnp.arange(pair_count, dtype=jnp.int32))
    )
    token_of_slot = pair_of_slot // TOP
    padded_rows = jnp.concatenate([normed_two, jnp.zeros((1, width), jnp.bfloat16)], axis=0)
    send_rows = jnp.take(padded_rows, token_of_slot, axis=0)
    routed_expert_rows = lax.all_to_all(
        spread_copies(send_rows, groups, shards),
        ("expert", "shard"),
        split_axis=0,
        concat_axis=0,
        tiled=True,
    ).reshape(devices, EXP_DEV, capacity, width)
    gate_preactivation = jnp.einsum(
        "sjcd,jdf->sjcf", routed_expert_rows, e_gate, preferred_element_type=jnp.float32
    )
    up_preactivation = jnp.einsum(
        "sjcd,jdf->sjcf", routed_expert_rows, expert_up_weight, preferred_element_type=jnp.float32
    )
    inner_act = (jax.nn.silu(gate_preactivation) * up_preactivation).astype(jnp.bfloat16)
    partial_out = jnp.einsum(
        "sjcf,jfd->sjcd", inner_act, e_down, preferred_element_type=jnp.float32
    )
    shared_gate = matmul(normed_two, full_sgate)
    shared_upper = matmul(normed_two, full_sup)
    shared_inner = (jax.nn.silu(shared_gate) * shared_upper).astype(jnp.bfloat16)
    shared_result = matmul(shared_inner, full_sdown)
    returned = lax.all_to_all(
        partial_out.reshape(devices * EXP_DEV * capacity, width),
        ("expert", "shard"),
        split_axis=0,
        concat_axis=0,
        tiled=True,
    )
    expert_sum = fold_slices(returned, groups, shards).astype(jnp.bfloat16)
    picked = (
        jnp.take(expert_sum, slot_of, axis=0).reshape(tokens_here, TOP, width).astype(jnp.float32)
    )
    routed = jnp.sum(route_weights[:, :, None] * picked, axis=1)
    output_rows = residual_mid + routed + shared_result
    grad_top = cotangent[0]
    grad_top_f = grad_top.astype(jnp.float32)
    grad_pairs = (
        (route_weights[:, :, None] * grad_top_f[:, None, :])
        .astype(jnp.bfloat16)
        .reshape(pair_count, width)
    )
    grad_padded = jnp.concatenate([grad_pairs, jnp.zeros((1, width), jnp.bfloat16)], axis=0)
    grad_send = jnp.take(grad_padded, pair_of_slot, axis=0)
    grad_expert_rows = lax.all_to_all(
        spread_copies(grad_send, groups, shards),
        ("expert", "shard"),
        split_axis=0,
        concat_axis=0,
        tiled=True,
    ).reshape(devices, EXP_DEV, capacity, width)
    grad_shared_inner = outer_cols(grad_top, full_sdown)
    grad_sgate_b, grad_sup_b = swish_gradients(shared_gate, shared_upper, grad_shared_inner)
    grad_normed_two = outer_cols(grad_sgate_b, full_sgate) + outer_cols(grad_sup_b, full_sup)
    grad_weights = jnp.sum(grad_top_f[:, None, :] * picked, axis=-1)
    grad_chosen = ROUTE_SCALE * (
        grad_weights / chosen_total
        - jnp.sum(grad_weights * chosen, axis=1, keepdims=True) / (chosen_total * chosen_total)
    )
    grad_probs = jnp.sum(jnp.where(choose, grad_chosen[:, :, None], 0.0), axis=1)
    grad_logits = (grad_probs * probs_r * (1.0 - probs_r)).astype(jnp.bfloat16)
    grad_normed_two = grad_normed_two + outer_cols(grad_logits, full_router)
    grad_inner_hidden = jnp.einsum(
        "sjcd,jfd->sjcf", grad_expert_rows, e_down, preferred_element_type=jnp.float32
    )
    d_edown = jnp.einsum(
        "sjcf,sjcd->jfd", inner_act, grad_expert_rows, preferred_element_type=jnp.float32
    )
    grad_expert_gate_batch, grad_expert_up_batch = swish_gradients(
        gate_preactivation, up_preactivation, grad_inner_hidden
    )
    d_egate = jnp.einsum(
        "gbvp,gbvq->bpq",
        routed_expert_rows,
        grad_expert_gate_batch,
        preferred_element_type=jnp.float32,
    )
    grad_expert_up = jnp.einsum(
        "gbvp,gbvq->bpq",
        routed_expert_rows,
        grad_expert_up_batch,
        preferred_element_type=jnp.float32,
    )
    grad_rows_part = jnp.einsum(
        "zukg,uyg->zuky", grad_expert_gate_batch, e_gate, preferred_element_type=jnp.float32
    ) + jnp.einsum(
        "zukg,uyg->zuky", grad_expert_up_batch, expert_up_weight, preferred_element_type=jnp.float32
    )
    grad_returned = lax.all_to_all(
        grad_rows_part.reshape(devices * EXP_DEV * capacity, width),
        ("expert", "shard"),
        split_axis=0,
        concat_axis=0,
        tiled=True,
    )
    grad_rows_sum = fold_slices(grad_returned, groups, shards).astype(jnp.bfloat16)
    grad_from_experts = jnp.sum(
        jnp.take(grad_rows_sum, slot_of, axis=0)
        .reshape(tokens_here, TOP, width)
        .astype(jnp.float32),
        axis=1,
    )
    grad_normed_two = grad_normed_two + grad_from_experts
    grad_mid_norm, d_gffn = norm_backward(grad_normed_two, second_norm_gain, unit_two, factor_two)
    grad_mid = grad_top_f + grad_mid_norm
    grad_attn_b = grad_mid.astype(jnp.bfloat16)
    grad_attended = (
        outer_cols(grad_attn_b, full_out).astype(jnp.bfloat16).reshape(tokens_here, H, DV)
    )
    scores_again = masked_scores()
    weights_again = jnp.exp(scores_again - log_total)
    grad_weights_attn = jnp.einsum(
        "qhd,khd->hqk", grad_attended, values_all, preferred_element_type=jnp.float32
    )
    row_delta = jnp.sum(weights_again * grad_weights_attn, axis=-1, keepdims=True)
    grad_scores = (weights_again * (grad_weights_attn - row_delta) * score_scale).astype(
        jnp.bfloat16
    )
    grad_query_nope = jnp.einsum(
        "hqk,khd->qhd", grad_scores, key_nope, preferred_element_type=jnp.float32
    )
    grad_query_rope = jnp.einsum(
        "hqk,kd->qhd", grad_scores, key_rope, preferred_element_type=jnp.float32
    )
    grad_key_nope = jnp.einsum(
        "hqk,qhd->khd", grad_scores, query_in[..., :DN], preferred_element_type=jnp.float32
    )
    grad_values = jnp.einsum(
        "hqk,qhd->khd",
        weights_again.astype(jnp.bfloat16),
        grad_attended,
        preferred_element_type=jnp.float32,
    )
    grad_key_rope = jnp.einsum(
        "hqk,qhd->kd", grad_scores, query_in[..., DN:], preferred_element_type=jnp.float32
    )
    grad_expanded = (
        jnp.concatenate([grad_key_nope, grad_values], axis=-1)
        .reshape(key_count, H * (DN + DV))
        .astype(jnp.bfloat16)
    )
    d_expand = inner_rows(latent_all[:, :KVR], grad_expanded)
    grad_latent_all = jnp.concatenate(
        [outer_cols(grad_expanded, full_expand), grad_key_rope], axis=1
    )
    grad_latent = lax.psum_scatter(grad_latent_all, "shard", scatter_dimension=0, tiled=True)
    grad_comp_norm, d_glatent = norm_backward(
        grad_latent[:, :KVR], glatent, latent_unit, latent_factor
    )
    grad_comp_rope = rotate(grad_latent[:, KVR:], cos_local, -sin_local)
    grad_compressed = jnp.concatenate([grad_comp_norm, grad_comp_rope], axis=1).astype(jnp.bfloat16)
    grad_query = (
        jnp.concatenate(
            [
                grad_query_nope,
                rotate(grad_query_rope, cos_local[:, None, :], -sin_local[:, None, :]),
            ],
            axis=-1,
        )
        .reshape(tokens_here, H * (DN + DR))
        .astype(jnp.bfloat16)
    )
    grad_normed = outer_cols(grad_compressed, full_latent) + outer_cols(grad_query, full_query)
    grad_input_norm, d_gattn = norm_backward(grad_normed, first_norm_gain, unit_one, factor_one)
    grad_input = grad_mid + grad_input_norm
    (
        normed_cols,
        normed_two_cols,
        attended_cols,
        inner_cols,
        query_grads,
        latent_grads,
        attn_grads,
        logit_grads,
        sgate_grads,
        sup_grads,
        top_grads,
    ) = (
        lax.all_to_all(
            column_pieces(normed, shards), "shard", split_axis=1, concat_axis=0, tiled=True
        ),
        lax.all_to_all(
            column_pieces(normed_two, shards), "shard", split_axis=1, concat_axis=0, tiled=True
        ),
        lax.all_to_all(
            column_pieces(attended, shards), "shard", split_axis=1, concat_axis=0, tiled=True
        ),
        lax.all_to_all(
            column_pieces(shared_inner, shards), "shard", split_axis=1, concat_axis=0, tiled=True
        ),
        lax.all_to_all(
            full_copies(grad_query, shards), "shard", split_axis=1, concat_axis=0, tiled=True
        ),
        lax.all_to_all(
            full_copies(grad_compressed, shards), "shard", split_axis=1, concat_axis=0, tiled=True
        ),
        lax.all_to_all(
            full_copies(grad_attn_b, shards), "shard", split_axis=1, concat_axis=0, tiled=True
        ),
        lax.all_to_all(
            full_copies(grad_logits, shards), "shard", split_axis=1, concat_axis=0, tiled=True
        ),
        lax.all_to_all(
            full_copies(grad_sgate_b, shards), "shard", split_axis=1, concat_axis=0, tiled=True
        ),
        lax.all_to_all(
            full_copies(grad_sup_b, shards), "shard", split_axis=1, concat_axis=0, tiled=True
        ),
        lax.all_to_all(
            full_copies(grad_top, shards), "shard", split_axis=1, concat_axis=0, tiled=True
        ),
    )
    rows_query = inner_rows(normed_cols[:, 0], query_grads[:, 0])
    rows_latent = inner_rows(normed_cols[:, 0], latent_grads[:, 0])
    rows_out = inner_rows(attended_cols[:, 0], attn_grads[:, 0])
    rows_router = inner_rows(normed_two_cols[:, 0], logit_grads[:, 0])
    rows_sgate = inner_rows(normed_two_cols[:, 0], sgate_grads[:, 0])
    rows_sup = inner_rows(normed_two_cols[:, 0], sup_grads[:, 0])
    rows_sdown = inner_rows(inner_cols[:, 0], top_grads[:, 0])
    rows_expand, rows_glatent, rows_gattn, rows_gffn = (
        lax.psum_scatter(d_expand, "shard", scatter_dimension=0, tiled=True),
        lax.psum_scatter(d_glatent, "shard", scatter_dimension=0, tiled=True),
        lax.psum_scatter(d_gattn, "shard", scatter_dimension=0, tiled=True),
        lax.psum_scatter(d_gffn, "shard", scatter_dimension=0, tiled=True),
    )
    (
        part_query,
        part_latent,
        part_glatent,
        part_expand,
        part_out,
        part_gattn,
        part_gffn,
        part_router,
        part_sgate,
        part_sup,
        part_sdown,
    ) = lax.psum(
        (
            rows_query,
            rows_latent,
            rows_glatent,
            rows_expand,
            rows_out,
            rows_gattn,
            rows_gffn,
            rows_router,
            rows_sgate,
            rows_sup,
            rows_sdown,
        ),
        "expert",
    )
    return (
        output_rows.astype(jnp.bfloat16)[None],
        grad_input[None],
        part_query,
        part_latent,
        part_glatent,
        part_expand,
        part_out,
        part_gattn,
        part_gffn,
        part_router,
        part_sgate,
        part_sup,
        part_sdown,
        d_egate,
        grad_expert_up,
        d_edown,
    )


def solution(mesh):
    return jax.shard_map(
        body,
        mesh=mesh,
        in_specs=(
            P("expert", "shard", None),
            P("expert", "shard", None),
            P("expert", None),
            P("expert", "shard", None),
            P("shard", None),
            P("shard", None),
            P("shard"),
            P("shard", None),
            P("shard", None),
            P("shard"),
            P("shard"),
            P("shard", None),
            P("shard", None),
            P("shard", None),
            P("shard", None),
            P("expert", None, "shard"),
            P("expert", None, "shard"),
            P("expert", "shard", None),
        ),
        out_specs=(
            P("expert", "shard", None),
            P("expert", "shard", None),
            P("shard", None),
            P("shard", None),
            P("shard"),
            P("shard", None),
            P("shard", None),
            P("shard"),
            P("shard"),
            P("shard", None),
            P("shard", None),
            P("shard", None),
            P("shard", None),
            P("expert", None, "shard"),
            P("expert", None, "shard"),
            P("expert", "shard", None),
        ),
        check_vma=False,
    )
```

profile of v0, /device:TPU:0, one launch (start us, length us, event | category | flops | bytes accessed | tf_op | source)
XLA Modules:
  0.0 3939.9 jit_solution(10518524136840859109)
XLA Ops:
  32.0 8.3 mul.462
  56.4 11.4 all_gather.39
  67.8 8.6 all-gather.13.cloned.1.call-done
  89.4 70.6 %all-gather.15.cloned.1.call-done = bf16[2048,3072]{1,0:T(8,128)(2,1)} async-done(((bf16[512,3072]{1,0:T(8,128)(2,1)}), bf16[2048,3072]{1,0:T(8,128)(2,1)}) %all-gather.15.cloned.1.call-update) | async-done | bytes 12582928 | tf_op jit(solution)/shard_map/all_gather | solution.py:154
  160.1 16.8 copy.116
  191.3 28.5 all-gather.17.cloned.1.call-done
  232.5 11.1 gather_fusion.1
  255.6 367.8 %all_to_all.201 = bf16[32,128,2048]{2,1,0:T(8,128)(2,1)} all-to-all(bf16[32,128,2048]{2,1,0:T(8,128)(2,1)S(1)} %bitcast.354), channel_id=1, replica_groups=mesh['expert'=8,'shard'=4] {'expert','shard'}, dimensions={0} | all-to-all | bytes 33554432 | tf_op jit(solution)/shard_map/all_to_all | solution.py:243
  634.0 15.9 fusion.5
  649.8 14.1 fusion.7
  663.9 342.7 %all-to-all-done.2 = bf16[32,128,2048]{2,1,0:T(8,128)(2,1)} async-done(((bf16[32,128,2048]{2,1,0:T(8,128)(2,1)}), bf16[32,128,2048]{2,1,0:T(8,128)(2,1)}, u32[]{:S(2)}, u32[]{:S(2)}) %all-to-all-start.2) | async-done | bytes 16777248 | tf_op jit(solution)/shard_map/all_to_all | solution.py:286
  1006.6 17.8 fusion.12
  1024.4 19.6 convolution_bitcast_fusion
  1043.9 23.2 copy.127
  1071.4 18.4 fusion.20
  1089.8 25.0 add_bitcast_fusion
  1114.8 23.1 copy.132
  1137.9 682.6 %all-to-all-done.1 = f32[32,128,2048]{2,1,0:T(8,128)} async-done(((f32[32,128,2048]{2,1,0:T(8,128)}), f32[32,128,2048]{2,1,0:T(8,128)}, u32[]{:S(2)}, u32[]{:S(2)}) %all-to-all-start.1) | async-done | bytes 33554464 | tf_op jit(solution)/shard_map/all_to_all | solution.py:264
  1827.1 270.6 %all-gather.19.cloned.1.call-done = bf16[2048,2816]{1,0:T(8,128)(2,1)} async-done(((bf16[512,2816]{1,0:T(8,128)(2,1)}), bf16[2048,2816]{1,0:T(8,128)(2,1)}) %all-gather.19.cloned.1.call-update) | async-done | bytes 11534352 | tf_op jit(solution)/shard_map/all_gather | solution.py:162
  2103.7 188.2 %all-gather.21.cloned.1.call-done = bf16[2048,2816]{1,0:T(8,128)(2,1)} async-done(((bf16[512,2816]{1,0:T(8,128)(2,1)}), bf16[2048,2816]{1,0:T(8,128)(2,1)}) %all-gather.21.cloned.1.call-update) | async-done | bytes 11534352 | tf_op jit(solution)/shard_map/all_gather | solution.py:163
  2298.9 97.4 %all-gather.23.cloned.1.call-done = bf16[2816,2048]{1,0:T(8,128)(2,1)} async-done(((bf16[704,2048]{1,0:T(8,128)(2,1)}), bf16[2816,2048]{1,0:T(8,128)(2,1)}) %all-gather.23.cloned.1.call-update) | async-done | bytes 11534352 | tf_op jit(solution)/shard_map/all_gather | solution.py:164
  2396.4 9.8 multiply_convert_fusion.2
  2406.2 8.6 fusion.168
  2419.6 15.5 bitcast_reduce_fusion.1
  2435.1 9.1 gather_fusion.2
  2448.3 139.7 %all-to-all-done.3 = f32[32,128,2048]{2,1,0:T(8,128)} async-done(((f32[32,128,2048]{2,1,0:T(8,128)}), f32[32,128,2048]{2,1,0:T(8,128)}, u32[]{:S(2)}, u32[]{:S(2)}) %all-to-all-start.3) | async-done | bytes 33554464 | tf_op jit(solution)/shard_map/all_to_all | solution.py:330
  2588.1 15.1 bitcast_reduce_fusion
  2603.2 9.8 gather_fusion.3
  2653.7 19.9 convert_bitcast_fusion.1
  2673.5 17.5 fusion.84
  2697.3 8.2 fusion.121
  2707.1 16.4 all_to_all.202
  2723.8 28.9 all_to_all.203
  2757.1 14.0 all-to-all-done.7
  2776.7 12.6 all-to-all-done.9
  2789.3 23.3 all_to_all.204
  2814.0 37.4 all_to_all.205
  2851.7 37.4 all_to_all.206
  2901.9 20.5 fusion.79
  2932.7 18.6 fusion.76
  2984.8 13.7 all-to-all-done.5
  3006.7 13.3 convolution_bitcast_fusion.1
  3020.0 13.2 convolution_bitcast_fusion.2
  3033.2 13.4 fusion.25
  3046.6 8.1 reshape.577
  3078.3 11.7 all-reduce.7
  3090.2 19.3 all-reduce.5
  3112.4 797.3 %all-reduce.10.cloned.1.call-done = (f32[512,3072]{1,0:T(8,128)}, f32[512,576]{0,1:T(8,128)}, f32[128,4096]{1,0:T(8,128)}, f32[512,2048]{1,0:T(8,128)}, f32[512,...) async-done(((f32[512,3072]{1,0:T(8,128)}, f32[512,576]{0,1:T(8,128)}, f32[128,4096]{1,0:T(8,128)}, f32[512,2048]{1,0:T(8,128)}, ...) | async-done | bytes 31129616 | tf_op jit(solution)/shard_map/psum | solution.py:479
  (406 shorter events, 308.5 us)
Async XLA Ops:
  7.2 45.8 %all-gather.11.cloned.1.call-start = ((), (), s32[]{:S(2)}) async-start(), calls=%async_computation.17 | async-start | bytes 2949120 | tf_op jit(solution)/shard_map/all_gather | solution.py:155
  8.0 68.4 %all-gather.13.cloned.1.call-start = ((), (), s32[]{:S(2)}) async-start(), calls=%async_computation.18 | async-start | bytes 5242880 | tf_op jit(solution)/shard_map/all_gather | solution.py:157
  8.7 151.3 %all-gather.15.cloned.1.call-start = ((), (), s32[]{:S(2)}) async-start(), calls=%async_computation.19 | async-start | bytes 15728640 | tf_op jit(solution)/shard_map/all_gather | solution.py:154
  9.5 210.3 %all-gather.17.cloned.1.call-start = ((), (), s32[]{:S(2)}) async-start(), calls=%async_computation.20 | async-start | bytes 10485760 | tf_op jit(solution)/shard_map/all_gather | solution.py:158
  10.1 216.1 %copy-start.69 = (s32[1,128,6]{1,2,0:T(8,128)}, s32[1,128,6]{1,2,0:T(8,128)S(1)}, u32[]{:S(2)}) copy-start(s32[1,128,6]{1,2,0:T(8,128)S(1)} %copy.197) | copy-start | bytes 9220
  10.5 32.2 copy-start.65
  16.7 160.2 %copy-start.51 = (f32[4,1,512]{2,1,0:T(1,128)}, f32[4,1,512]{2,1,0:T(1,128)S(1)}, u32[]{:S(2)}) copy-start(f32[4,1,512]{2,1,0:T(1,128)S(1)} %convert_element_type.214) | copy-start | bytes 24580
  22.0 33.8 copy-start.73
  27.5 197.3 %copy-start.53 = (f32[4,1,512]{2,1,0:T(1,128)}, f32[4,1,512]{2,1,0:T(1,128)S(1)}, u32[]{:S(2)}) copy-start(f32[4,1,512]{2,1,0:T(1,128)S(1)} %convert_element_type.216) | copy-start | bytes 24580
  32.0 20.6 copy-start.91
  32.0 20.6 copy-start.8
  52.5 173.3 %copy-start.41 = (bf16[2048,32]{0,1:T(8,128)(2,1)}, bf16[2048,32]{0,1:T(8,128)(2,1)S(1)}, u32[]{:S(2)}) copy-start(bf16[2048,32]{0,1:T(8,128)(2,1)S(1)} %all_gather.44) | copy-start | bytes 393220
  52.8 124.1 %copy-start.80 = (f32[128]{0:T(128)}, f32[128]{0:T(128)S(1)}, u32[]{:S(2)}) copy-start(f32[128]{0:T(128)S(1)} %add_rsqrt_fusion.2) | copy-start | bytes 1540
  55.8 127.7 %copy-start.56 = (f32[128,32]{0,1:T(8,128)}, f32[128,32]{0,1:T(8,128)S(1)}, u32[]{:S(2)}) copy-start(f32[128,32]{0,1:T(8,128)S(1)} %get-tuple-element.64) | copy-start | bytes 49156
  67.8 117.1 %copy-start.24 = (bf16[512,576]{0,1:T(8,128)(2,1)}, bf16[512,576]{0,1:T(8,128)(2,1)S(1)}, u32[]{:S(2)}) copy-start(bf16[512,576]{0,1:T(8,128)(2,1)S(1)} %all_gather.39) | copy-start | bytes 1769476
  84.4 99.2 %copy-start.18 = (bf16[512,16,128]{2,1,0:T(8,128)(2,1)}, bf16[512,16,128]{2,1,0:T(8,128)(2,1)S(1)}, u32[]{:S(2)}) copy-start(bf16[512,16,128]{2,1,0:T(8,128)(2,1)S(1)} %get-tuple-element.44) | copy-start | bytes 6291460
  629.5 377.1 %all-to-all-start.2 = ((bf16[32,128,2048]{2,1,0:T(8,128)(2,1)}), bf16[32,128,2048]{2,1,0:T(8,128)(2,1)}, u32[]{:S(2)}, u32[]{:S(2)}) async-start(bf16[32,128,2048]{2,1,0:T(8,128)(2,1)} %bitcast.353), calls=%async_computation.2 | async-start | bytes 33554432 | tf_op jit(solution)/shard_map/all_to_all | solution.py:286
  1024.4 65.5 %copy-start.34 = (bf16[32,4,32,352]{3,2,0,1:T(8,128)(2,1)}, bf16[32,4,32,352]{3,2,0,1:T(8,128)(2,1)S(1)}, u32[]{:S(2)}) copy-start(bf16[32,4,32,352]{3,2,0,1:T(8,128)(2,1)S(1)} %get-tuple-element.41) | copy-start | bytes 8650756
  1067.1 753.4 %all-to-all-start.1 = ((f32[32,128,2048]{2,1,0:T(8,128)}), f32[32,128,2048]{2,1,0:T(8,128)}, u32[]{:S(2)}, u32[]{:S(2)}) async-start(f32[32,128,2048]{2,1,0:T(8,128)} %bitcast.350), calls=%async_computation.1 | async-start | bytes 67108864 | tf_op jit(solution)/shard_map/all_to_all | solution.py:264
  1820.5 767.5 %all-to-all-start.3 = ((f32[32,128,2048]{2,1,0:T(8,128)}), f32[32,128,2048]{2,1,0:T(8,128)}, u32[]{:S(2)}, u32[]{:S(2)}) async-start(f32[32,128,2048]{2,1,0:T(8,128)} %bitcast.349), calls=%async_computation.3 | async-start | bytes 67108864 | tf_op jit(solution)/shard_map/all_to_all | solution.py:330
  1824.9 272.9 %copy-start.6 = (bf16[128,2048]{1,0:T(8,128)(2,1)S(1)}, bf16[128,2048]{1,0:T(8,128)(2,1)}, u32[]{:S(2)}) copy-start(bf16[128,2048]{1,0:T(8,128)(2,1)} %copy-done.5) | copy-start | bytes 1572868
  1824.9 272.9 %all-gather.19.cloned.1.call-start = ((), (), s32[]{:S(2)}) async-start(), calls=%async_computation.21 | async-start | bytes 14417920 | tf_op jit(solution)/shard_map/all_gather | solution.py:162
  1825.5 466.4 %all-gather.21.cloned.1.call-start = ((), (), s32[]{:S(2)}) async-start(), calls=%async_computation.22 | async-start | bytes 14417920 | tf_op jit(solution)/shard_map/all_gather | solution.py:163
  1826.0 570.3 %all-gather.23.cloned.1.call-start = ((), (), s32[]{:S(2)}) async-start(), calls=%async_computation.23 | async-start | bytes 14417920 | tf_op jit(solution)/shard_map/all_gather | solution.py:164
  1826.8 1095.6 %reduce-scatter.3.cloned.1.call-start = ((), (), s32[]{:S(2)}) async-start(), calls=%async_computation.24 | async-start | bytes 1474560 | tf_op jit(solution)/shard_map/reduce_scatter | solution.py:387
  2103.7 292.6 %copy-start.16 = (bf16[1,128,2048]{2,1,0:T(8,128)(2,1)S(1)}, bf16[1,128,2048]{2,1,0:T(8,128)(2,1)}, u32[]{:S(2)}) copy-start(bf16[1,128,2048]{2,1,0:T(8,128)(2,1)} %param.21) | copy-start | bytes 1572868
  2697.3 306.8 %reduce-scatter.5.cloned.1.call-start = ((), (), s32[]{:S(2)}) async-start(), calls=%async_computation.25 | async-start | bytes 10485760 | tf_op jit(solution)/shard_map/reduce_scatter | solution.py:462
  2723.5 32.7 copy-start.7
  2752.7 18.3 all-to-all-start.7
  2771.0 43.0 %copy-start.39 = (bf16[128,4,512]{0,2,1:T(8,128)(2,1)}, bf16[128,4,512]{0,2,1:T(8,128)(2,1)S(1)}, u32[]{:S(2)}) copy-start(bf16[128,4,512]{0,2,1:T(8,128)(2,1)S(1)} %all-to-all-done.7) | copy-start | bytes 1572868
  2771.0 18.3 all-to-all-start.9
  2812.6 38.9 copy-start.37
  2851.5 43.9 %copy-start.27 = (bf16[128,2048]{1,0:T(8,128)(2,1)S(1)}, bf16[128,2048]{1,0:T(8,128)(2,1)}, u32[]{:S(2)}) copy-start(bf16[128,2048]{1,0:T(8,128)(2,1)} %copy-done.26) | copy-start | bytes 1572868
  2897.0 30.6 all-to-all-start.8
  2901.8 20.5 copy-start.22
  2901.8 20.5 copy-start.74
  2901.9 20.5 copy-start.88
  2901.9 21.7 copy-start.93
  2901.9 21.7 copy-start.95
  2925.6 25.7 copy-start.57
  2928.4 24.0 copy-start.50
  2928.4 25.2 all-to-all-start.6
  2956.9 41.6 %all-to-all-start.5 = ((bf16[128,4,3072]{2,0,1:T(8,128)(2,1)}), bf16[128,4,3072]{2,0,1:T(8,128)(2,1)}, u32[]{:S(2)}, u32[]{:S(2)}) async-start(bf16[128,4,3072]{2,0,1:T(8,128)(2,1)} %broadcast_in_dim.114), calls=%async_computation.6 | async-start | bytes 6291456 | tf_op jit(solution)/shard_map/all_to_all | solution.py:432
  2961.5 948.2 %all-reduce.10.cloned.1.call-start = ((), (), s32[]{:S(2)}) async-start(), calls=%async_computation.26 | async-start | bytes 62259200 | tf_op jit(solution)/shard_map/psum | solution.py:479
  3074.5 35.0 copy-start.14
  3074.5 35.0 copy-start.55
  3074.5 35.0 copy-start.84
  3074.5 35.0 copy-start.90
  (84 other events, 546.2 us)
Sparse Core Ops, SparseCore 0:
  9.6 26.7 all-gather.10
  38.0 38.3 all-gather.12
  77.9 82.0 all-gather.14
  161.5 58.2 all-gather.16
  1826.9 270.7 all-gather.18
  2099.2 192.6 all-gather.20
  2293.4 102.8 all-gather.22
  2697.4 26.0 reduce-scatter.2
  2726.7 92.1 reduce-scatter.4
  3004.2 905.4 all-reduce.9
where the time goes:
time: 3950 us; the launch traced here: 3940 us
  waiting for transfers between devices  2670 us (68%)
  blocking collectives  583 us (15%)
  matrix products  356 us (9%)
  local copies, waits for them, and re-layouts  197 us (5%)
  other arithmetic  78.5 us (2%)
    psum x1, waiting for transfers between devices, body(): lax.psum((rows_query, rows_latent, rows_glatent, rows_expand, rows_out, r...  797 us
    all_to_all x1, waiting for transfers between devices, body(): lax.all_to_all(partial_out.reshape(devices * EXP_DEV * capacity, width),...  683 us
    all_to_all x1, blocking collectives, body(): lax.all_to_all(spread_copies(send_rows, groups, shards), ('expert', 'shar...  368 us
    all_to_all x1, waiting for transfers between devices, body(): lax.all_to_all(spread_copies(grad_send, groups, shards), ('expert', 'shar...  343 us
    all_gather x1, waiting for transfers between devices, body(): lax.all_gather(s_gate, 'shard', axis=0, tiled=True)  271 us
    all_gather x1, waiting for transfers between devices, body(): lax.all_gather(s_up, 'shard', axis=0, tiled=True)  188 us
    all_to_all x1, waiting for transfers between devices, body(): lax.all_to_all(grad_rows_part.reshape(devices * EXP_DEV * capacity, width...  140 us
    all_gather x1, waiting for transfers between devices, body(): lax.all_gather(s_down, 'shard', axis=0, tiled=True)  97.4 us
  transfers between devices with their start and end apart: 18, of which 14 were waited for; matrix products, arithmetic and copies ran while one was open for 10% of the time, Pallas kernels for 0%

commit v1 on v0

v1 whole, which is shorter than its diff:
```python
import functools

import jax
import jax.numpy as jnp
from jax import lax
from jax.experimental import pallas as pl
from jax.experimental.pallas import tpu as pltpu
from jax.sharding import PartitionSpec as P

H = 16
DN = 128
DR = 64
DV = 128
KVR = 512
TOP = 6
EXP_DEV = 4

EPS = 1e-06
ROUTE_SCALE = 2.446
ROPE_BASE = 50000.0
SCORE_SCALE = (DN + DR) ** (-0.5)
BF = jnp.bfloat16
F32 = jnp.float32
BOTH = ("expert", "shard")
VMEM_BYTES = 56 * 1024 * 1024


def mm(a, b):
    return jnp.dot(a, b, preferred_element_type=F32)


def mm_tn(a, b):
    return lax.dot_general(a, b, (((0,), (0,)), ((), ())), preferred_element_type=F32)


def mm_nt(a, b):
    return lax.dot_general(a, b, (((1,), (1,)), ((), ())), preferred_element_type=F32)


def rope_angles(positions):
    half_width = DR // 2
    inverse = ROPE_BASE ** (-jnp.arange(half_width).astype(F32) / half_width)
    angles = positions.astype(F32)[:, None] * inverse[None, :]
    return (jnp.cos(angles), jnp.sin(angles))


def rotate(values, cosine, sine_vals):
    half_width = DR // 2
    first_half = values[..., :half_width]
    second_half = values[..., half_width:]
    return jnp.concatenate(
        [
            first_half * cosine - second_half * sine_vals,
            second_half * cosine + first_half * sine_vals,
        ],
        axis=-1,
    )


def norm_forward(values):
    factor = lax.rsqrt(jnp.mean(values * values, axis=-1, keepdims=True) + EPS)
    return values * factor, factor


def norm_backward(grad_out, gain_vec, unit_vals, factor):
    grad_unit = grad_out * gain_vec
    grad_in = factor * (
        grad_unit - unit_vals * jnp.mean(grad_unit * unit_vals, axis=-1, keepdims=True)
    )
    return (grad_in, jnp.sum(grad_out * unit_vals, axis=0))


def swish_parts(gate, up):
    sig = jax.nn.sigmoid(gate)
    silu = gate * sig
    return silu * up, up * sig * (1.0 + gate * (1.0 - sig)), silu


def exchange(values, axis):
    return lax.all_to_all(values, axis, split_axis=0, concat_axis=0, tiled=True)


def gather_shard(values, shards):
    copies = jnp.broadcast_to(values[None], (shards,) + values.shape)
    got = exchange(copies, "shard")
    return got.reshape((shards * values.shape[0],) + values.shape[1:])


def sum_shard(values, shards):
    rows = values.shape[0] // shards
    got = exchange(values.reshape((shards, rows) + values.shape[1:]), "shard")
    return jnp.sum(got.astype(F32), axis=0)


def params(**kw):
    return pltpu.CompilerParams(vmem_limit_bytes=VMEM_BYTES, **kw)


def allowed_mask(seg_col, seg_row):
    length = seg_row.shape[1]
    rows = lax.broadcasted_iota(jnp.int32, (length, length), 0)
    cols = lax.broadcasted_iota(jnp.int32, (length, length), 1)
    return (seg_col == seg_row) & (cols <= rows)


def attention_forward_kernel(
    n1_ref, wq_ref, lat_ref, we_ref, cos_ref, sin_ref, segc_ref, segr_ref,
    o_ref, q_ref, kv_ref, lse_ref,
):
    width = n1_ref.shape[1]
    query = mm(n1_ref[...], wq_ref[...].reshape(width, DN + DR))
    query = jnp.concatenate(
        [query[:, :DN], rotate(query[:, DN:], cos_ref[...], sin_ref[...])], axis=1
    ).astype(BF)
    q_ref[0] = query
    kv = mm(lat_ref[:, :KVR], we_ref[...].reshape(KVR, DN + DV)).astype(BF)
    kv_ref[0] = kv
    scores = mm_nt(query[:, :DN], kv[:, :DN]) + mm_nt(query[:, DN:], lat_ref[:, KVR:])
    ok = allowed_mask(segc_ref[...], segr_ref[...])
    scores = jnp.where(ok, scores * SCORE_SCALE, -1e30)
    top = jnp.max(scores, axis=1, keepdims=True)
    expo = jnp.exp(scores - top)
    total = jnp.sum(expo, axis=1, keepdims=True)
    lse_ref[0] = top + jnp.log(total)
    weights = (expo / total).astype(BF)
    o_ref[...] = mm(weights, kv[:, DN:]).astype(BF)


def attention_forward(n1, wq, latent, we, cosine, sine_vals, seg_col, seg_row):
    length, width = n1.shape
    shards, heads = wq.shape[0], wq.shape[1]
    whole = lambda shape: pl.BlockSpec(shape, lambda h: (0,) * len(shape))
    return pl.pallas_call(
        attention_forward_kernel,
        grid=(heads,),
        in_specs=[
            whole((length, width)),
            pl.BlockSpec((shards, 1, width // shards, DN + DR), lambda h: (0, h, 0, 0)),
            whole((length, KVR + DR)),
            pl.BlockSpec((shards, 1, KVR // shards, DN + DV), lambda h: (0, h, 0, 0)),
            whole((length, DR // 2)),
            whole((length, DR // 2)),
            whole((length, 1)),
            whole((1, length)),
        ],
        out_specs=[
            pl.BlockSpec((length, DV), lambda h: (0, h)),
            pl.BlockSpec((1, length, DN + DR), lambda h: (h, 0, 0)),
            pl.BlockSpec((1, length, DN + DV), lambda h: (h, 0, 0)),
            pl.BlockSpec((1, length, 1), lambda h: (h, 0, 0)),
        ],
        out_shape=[
            jax.ShapeDtypeStruct((length, heads * DV), BF),
            jax.ShapeDtypeStruct((heads, length, DN + DR), BF),
            jax.ShapeDtypeStruct((heads, length, DN + DV), BF),
            jax.ShapeDtypeStruct((heads, length, 1), F32),
        ],
        compiler_params=params(),
        name="attention_forward",
    )(n1, wq, latent, we, cosine, sine_vals, seg_col, seg_row)


def attention_backward_kernel(
    dh_ref, wo_ref, o_ref, q_ref, kv_ref, lse_ref, lat_ref, we_ref, wq_ref, n1_ref,
    cos_ref, sin_ref, segc_ref, segr_ref,
    dn1_ref, dlat_ref, dwq_ref, dwe_ref, dwo_ref,
):
    head = pl.program_id(0)
    width = n1_ref.shape[1]
    shards = wq_ref.shape[0]
    query, kv = q_ref[0], kv_ref[0]
    grad_o = mm_nt(dh_ref[...], wo_ref[...]).astype(BF)
    dwo_ref[...] = mm_tn(o_ref[...], dh_ref[...]).astype(BF)
    scores = mm_nt(query[:, :DN], kv[:, :DN]) + mm_nt(query[:, DN:], lat_ref[:, KVR:])
    ok = allowed_mask(segc_ref[...], segr_ref[...])
    weights = jnp.where(ok, jnp.exp(scores * SCORE_SCALE - lse_ref[0]), 0.0)
    grad_w = mm_nt(grad_o, kv[:, DN:])
    delta = jnp.sum(weights * grad_w, axis=1, keepdims=True)
    grad_s = (weights * (grad_w - delta) * SCORE_SCALE).astype(BF)
    grad_qr = mm(grad_s, lat_ref[:, KVR:])
    grad_q = jnp.concatenate(
        [mm(grad_s, kv[:, :DN]), rotate(grad_qr, cos_ref[...], -sin_ref[...])], axis=1
    ).astype(BF)
    grad_kv = jnp.concatenate(
        [mm_tn(grad_s, query[:, :DN]), mm_tn(weights.astype(BF), grad_o)], axis=1
    ).astype(BF)
    grad_kr = mm_tn(grad_s, query[:, DN:])
    dwq_ref[...] = mm_tn(n1_ref[...], grad_q).astype(BF).reshape(dwq_ref.shape)
    dwe_ref[...] = mm_tn(lat_ref[:, :KVR], grad_kv).astype(BF).reshape(dwe_ref.shape)
    part_n1 = mm_nt(grad_q, wq_ref[...].reshape(width, DN + DR))
    part_lat = mm_nt(grad_kv, we_ref[...].reshape(KVR, DN + DV))

    @pl.when(head == 0)
    def _():
        dn1_ref[...] = part_n1
        dlat_ref[:, :KVR] = part_lat
        dlat_ref[:, KVR:] = grad_kr

    @pl.when(head > 0)
    def _():
        dn1_ref[...] += part_n1
        dlat_ref[:, :KVR] += part_lat
        dlat_ref[:, KVR:] += grad_kr


def attention_backward(
    dh, wo, o, query, kv, lse, latent, we, wq, n1, cosine, sine_vals, seg_col, seg_row
):
    length, width = n1.shape
    shards, heads = wq.shape[0], wq.shape[1]
    whole = lambda shape: pl.BlockSpec(shape, lambda h: (0,) * len(shape))
    wq_spec = pl.BlockSpec((shards, 1, width // shards, DN + DR), lambda h: (0, h, 0, 0))
    we_spec = pl.BlockSpec((shards, 1, KVR // shards, DN + DV), lambda h: (0, h, 0, 0))
    return pl.pallas_call(
        attention_backward_kernel,
        grid=(heads,),
        in_specs=[
            whole((length, width)),
            pl.BlockSpec((DV, width), lambda h: (h, 0)),
            pl.BlockSpec((length, DV), lambda h: (0, h)),
            pl.BlockSpec((1, length, DN + DR), lambda h: (h, 0, 0)),
            pl.BlockSpec((1, length, DN + DV), lambda h: (h, 0, 0)),
            pl.BlockSpec((1, length, 1), lambda h: (h, 0, 0)),
            whole((length, KVR + DR)),
            we_spec,
            wq_spec,
            whole((length, width)),
            whole((length, DR // 2)),
            whole((length, DR // 2)),
            whole((length, 1)),
            whole((1, length)),
        ],
        out_specs=[
            whole((length, width)),
            whole((length, KVR + DR)),
            wq_spec,
            we_spec,
            pl.BlockSpec((DV, width), lambda h: (h, 0)),
        ],
        out_shape=[
            jax.ShapeDtypeStruct((length, width), F32),
            jax.ShapeDtypeStruct((length, KVR + DR), F32),
            jax.ShapeDtypeStruct(wq.shape, BF),
            jax.ShapeDtypeStruct(we.shape, BF),
            jax.ShapeDtypeStruct((heads * DV, width), BF),
        ],
        compiler_params=params(),
        name="attention_backward",
    )(dh, wo, o, query, kv, lse, latent, we, wq, n1, cosine, sine_vals, seg_col, seg_row)


def pick_kernel(pick_ref, x_ref, out_ref):
    rows = mm(pick_ref[0], x_ref[0]).astype(BF)
    out_ref[...] = rows.reshape(out_ref.shape)


def pick_rows(pick, x_all, capacity):
    devices, slots, tokens = pick.shape
    width = x_all.shape[2]
    return pl.pallas_call(
        pick_kernel,
        grid=(devices,),
        in_specs=[
            pl.BlockSpec((1, slots, tokens), lambda d: (d, 0, 0)),
            pl.BlockSpec((1, tokens, width), lambda d: (d, 0, 0)),
        ],
        out_specs=pl.BlockSpec((EXP_DEV, capacity, width), lambda d: (0, d, 0)),
        out_shape=jax.ShapeDtypeStruct((EXP_DEV, devices * capacity, width), BF),
        compiler_params=params(),
        name="pick_rows",
    )(pick, x_all)


def place_kernel(pick_ref, rows_ref, left_ref, right_ref, out_ref):
    slots = pick_ref.shape[1]
    rows = rows_ref[...].reshape(slots, rows_ref.shape[2])
    total = mm_tn(pick_ref[0], rows) + mm(left_ref[0], right_ref[...])
    out_ref[0] = total.astype(BF)


def place_rows(pick, rows, left, right, capacity):
    devices, slots, tokens = pick.shape
    width = rows.shape[2]
    inner = left.shape[2]
    return pl.pallas_call(
        place_kernel,
        grid=(devices,),
        in_specs=[
            pl.BlockSpec((1, slots, tokens), lambda d: (d, 0, 0)),
            pl.BlockSpec((EXP_DEV, capacity, width), lambda d: (0, d, 0)),
            pl.BlockSpec((1, tokens, inner), lambda d: (d, 0, 0)),
            pl.BlockSpec((inner, width), lambda d: (0, 0)),
        ],
        out_specs=pl.BlockSpec((1, tokens, width), lambda d: (d, 0, 0)),
        out_shape=jax.ShapeDtypeStruct((devices, tokens, width), BF),
        compiler_params=params(),
        name="place_rows",
    )(pick, rows, left, right)


def body(
    hidden,
    cotangent,
    segments,
    routes,
    w_query,
    w_latent,
    g_latent,
    w_expand,
    w_out,
    g_attn,
    g_ffn,
    w_router,
    s_gate,
    s_up,
    s_down,
    e_gate,
    expert_up_weight,
    e_down,
):
    tokens = hidden.shape[1]
    width = hidden.shape[2]
    shards = lax.axis_size("shard")
    groups = lax.axis_size("expert")
    devices = groups * shards
    experts = EXP_DEV * groups
    capacity = max(2, tokens * TOP * 4 // (3 * experts))
    heads = H // shards
    length = tokens * shards
    part = width // shards
    my_shard = lax.axis_index("shard")
    my_group = lax.axis_index("expert")
    hid_shard = s_down.shape[0]
    hid = hid_shard // groups

    hidden_all = gather_shard(hidden[0], shards)
    wq = exchange(
        w_query.reshape(part, H, DN + DR).transpose(1, 0, 2), "shard"
    ).reshape(shards, heads, part, DN + DR)
    we = exchange(
        w_expand.reshape(KVR // shards, H, DN + DV).transpose(1, 0, 2), "shard"
    ).reshape(shards, heads, KVR // shards, DN + DV)
    full_latent = lax.all_gather(w_latent, "shard", axis=0, tiled=True)
    gain_pack = lax.all_gather(
        jnp.concatenate([g_attn, g_ffn, g_latent]), "shard", axis=0, tiled=False
    )
    gattn = gain_pack[:, :part].reshape(width).astype(F32)
    gffn = gain_pack[:, part : 2 * part].reshape(width).astype(F32)
    glatent = gain_pack[:, 2 * part :].reshape(KVR).astype(F32)
    full_router = lax.all_gather(w_router, "shard", axis=0, tiled=True)
    g_all = lax.all_gather(cotangent[0], BOTH, axis=0, tiled=False)

    mine = lambda w: lax.dynamic_slice_in_dim(
        w.reshape(part, shards, hid_shard), my_group * hid, hid, 2
    )
    gate_up = jnp.concatenate([mine(s_gate), mine(s_up)], axis=2).transpose(1, 0, 2)
    shared_in = exchange(gate_up, "shard").reshape(width, 2 * hid)
    shared_down = lax.dynamic_slice_in_dim(s_down, my_group * hid, hid, 0)

    local_routes = routes[0]
    flat_routes = local_routes.reshape(-1)
    choose = local_routes[:, :, None] == jnp.arange(experts, dtype=jnp.int32)[None, None, :]
    hits = choose.reshape(-1, experts).astype(F32)
    pair_count = tokens * TOP
    lower = (
        lax.broadcasted_iota(jnp.int32, (pair_count, pair_count), 1)
        < lax.broadcasted_iota(jnp.int32, (pair_count, pair_count), 0)
    ).astype(BF)
    before = mm(lower, hits.astype(BF))
    slot_rank = jnp.sum(before * hits, axis=1).astype(jnp.int32)
    slot_of = (flat_routes * capacity + slot_rank).reshape(tokens, TOP)
    slots = EXP_DEV * capacity
    slots_all = lax.all_gather(slot_of, BOTH, axis=0, tiled=False)
    slot_ids = my_group * slots + jnp.arange(slots, dtype=jnp.int32)
    match = slots_all[:, None, :, :] == slot_ids[None, :, None, None]
    pick = jnp.any(match, axis=3).astype(BF)

    residual_all = hidden_all.astype(F32)
    unit_all, factor_all = norm_forward(residual_all)
    n1 = (unit_all * gattn).astype(BF)
    cosine, sine_vals = rope_angles(jnp.arange(length, dtype=jnp.int32))
    compressed = mm(n1, full_latent)
    latent_unit, latent_factor = norm_forward(compressed[:, :KVR])
    latent = jnp.concatenate(
        [latent_unit * glatent, rotate(compressed[:, KVR:], cosine, sine_vals)], axis=1
    ).astype(BF)
    seg_row = segments
    seg_col = segments.reshape(length, 1)
    attended, query, kv, lse = attention_forward(
        n1, wq, latent, we, cosine, sine_vals, seg_col, seg_row
    )
    attn_out = sum_shard(mm(attended, w_out).astype(BF), shards)
    residual_in = hidden[0].astype(F32)
    residual_mid = residual_in + attn_out
    unit_two, factor_two = norm_forward(residual_mid)
    normed_two = (unit_two * gffn).astype(BF)

    n2_all = lax.all_gather(normed_two, BOTH, axis=0, tiled=False)
    probs = jax.nn.sigmoid(mm(normed_two, full_router))
    chosen = jnp.sum(jnp.where(choose, probs[:, None, :], 0.0), axis=-1)
    chosen_total = jnp.sum(chosen, axis=1, keepdims=True)
    route_weights = chosen / chosen_total * ROUTE_SCALE
    weights_all = lax.all_gather(route_weights, BOTH, axis=0, tiled=False)
    slot_weight = jnp.sum(
        jnp.where(match, weights_all[:, None, :, :], 0.0), axis=(2, 3)
    )
    by_expert = lambda v: v.reshape(devices, EXP_DEV, capacity).transpose(1, 0, 2).reshape(
        EXP_DEV, devices * capacity
    )
    row_weight = by_expert(slot_weight)[:, :, None]

    grad_rows = pick_rows(pick, g_all, capacity)
    grad_inner = jnp.einsum("jmd,jfd->jmf", grad_rows, e_down, preferred_element_type=F32)
    shared_grad_inner = mm_nt(g_all.reshape(-1, width), shared_down)
    rows = pick_rows(pick, n2_all, capacity)
    gate = jnp.einsum("jmd,jdf->jmf", rows, e_gate, preferred_element_type=F32)
    up = jnp.einsum("jmd,jdf->jmf", rows, expert_up_weight, preferred_element_type=F32)
    inner, slope_gate, slope_up = swish_parts(gate, up)
    weighted_grad = row_weight * grad_inner
    grad_gate_b = (weighted_grad * slope_gate).astype(BF)
    grad_up_b = (weighted_grad * slope_up).astype(BF)
    inner_w = (row_weight * inner).astype(BF)
    grad_slot_weight = jnp.sum(inner.astype(BF).astype(F32) * grad_inner, axis=2)

    shared_pre = mm(n2_all.reshape(-1, width), shared_in)
    s_inner, s_slope_gate, s_slope_up = swish_parts(shared_pre[:, :hid], shared_pre[:, hid:])
    shared_inner = s_inner.astype(BF)
    shared_grads = jnp.concatenate(
        [shared_grad_inner * s_slope_gate, shared_grad_inner * s_slope_up], axis=1
    ).astype(BF)

    dz = (
        jnp.einsum("jmf,jdf->jmd", grad_gate_b, e_gate, preferred_element_type=F32)
        + jnp.einsum("jmf,jdf->jmd", grad_up_b, expert_up_weight, preferred_element_type=F32)
    ).astype(BF)
    dn2_part = place_rows(
        pick, dz, shared_grads.reshape(devices, tokens, 2 * hid), shared_in.T, capacity
    )
    dn2 = lax.psum_scatter(dn2_part, BOTH, scatter_dimension=0, tiled=False).astype(F32)
    weighted_out = jnp.einsum(
        "jmf,jfd->jmd", inner_w, e_down, preferred_element_type=F32
    ).astype(BF)
    out_part = place_rows(
        pick, weighted_out, shared_inner.reshape(devices, tokens, hid), shared_down, capacity
    )
    routed_shared = lax.psum_scatter(
        out_part, BOTH, scatter_dimension=0, tiled=False
    ).astype(F32)
    output_rows = residual_mid + routed_shared

    d_edown = jnp.einsum("jmf,jmd->jfd", inner_w, grad_rows, preferred_element_type=F32)
    d_egate = jnp.einsum("jmd,jmf->jdf", rows, grad_gate_b, preferred_element_type=F32)
    grad_expert_up = jnp.einsum("jmd,jmf->jdf", rows, grad_up_b, preferred_element_type=F32)

    slot_back = grad_slot_weight.reshape(EXP_DEV, devices, capacity).transpose(1, 0, 2)
    got = exchange(slot_back.reshape(devices, slots), BOTH)
    slot_grads = jnp.sum(got.reshape(groups, shards, slots), axis=1).reshape(-1)
    at_slot = slot_of[:, :, None] == jnp.arange(experts * capacity, dtype=jnp.int32)
    grad_weights = jnp.sum(jnp.where(at_slot, slot_grads, 0.0), axis=2)
    grad_chosen = ROUTE_SCALE * (
        grad_weights / chosen_total
        - jnp.sum(grad_weights * chosen, axis=1, keepdims=True) / (chosen_total * chosen_total)
    )
    grad_probs = jnp.sum(jnp.where(choose, grad_chosen[:, :, None], 0.0), axis=1)
    grad_logits = (grad_probs * probs * (1.0 - probs)).astype(BF)

    d_shared_in = mm_tn(shared_grads, n2_all.reshape(-1, width)).astype(BF)
    d_shared_down = mm_tn(shared_inner, g_all.reshape(-1, width)).astype(BF)
    in_pieces = exchange(
        d_shared_in.reshape(2 * hid, shards, part).transpose(1, 0, 2), "shard"
    )
    in_all = lax.all_gather(in_pieces, "expert", axis=0, tiled=False)
    in_all = in_all.reshape(groups, shards, 2, hid, part).astype(F32)
    in_all = in_all.transpose(2, 1, 0, 3, 4).reshape(2, shards * groups * hid, part)
    part_sgate = in_all[0].T
    part_sup = in_all[1].T
    part_sdown = lax.all_gather(d_shared_down, "expert", axis=0, tiled=True).astype(F32)

    grad_normed_two = dn2 + mm_nt(grad_logits, full_router)
    grad_mid_norm, d_gffn = norm_backward(grad_normed_two, gffn, unit_two, factor_two)
    grad_mid = cotangent[0].astype(F32) + grad_mid_norm
    grad_attn = gather_shard(grad_mid.astype(BF), shards)
    d_router_part = mm_tn(normed_two, grad_logits)

    dn1_heads, dlat, dwq, dwe, d_out = attention_backward(
        grad_attn, w_out, attended, query, kv, lse, latent, we, wq, n1,
        cosine, sine_vals, seg_col, seg_row,
    )
    grad_comp_norm, d_glatent = norm_backward(dlat[:, :KVR], glatent, latent_unit, latent_factor)
    grad_compressed = jnp.concatenate(
        [grad_comp_norm, rotate(dlat[:, KVR:], cosine, -sine_vals)], axis=1
    ).astype(BF)
    grad_normed = sum_shard(
        (dn1_heads + mm_nt(grad_compressed, full_latent)).astype(BF), shards
    )
    unit_one, factor_one = norm_forward(residual_in)
    grad_input_norm, d_gattn = norm_backward(grad_normed, gattn, unit_one, factor_one)
    grad_input = grad_mid + grad_input_norm

    rows_query = exchange(dwq.reshape(H, part, DN + DR), "shard")
    rows_expand = exchange(dwe.reshape(H, KVR // shards, DN + DV), "shard")
    rows_latent = sum_shard(mm_tn(n1, grad_compressed).astype(BF), shards).astype(BF)
    sum_query, sum_latent, sum_expand, sum_out = lax.psum(
        (rows_query, rows_latent, rows_expand, d_out), "expert"
    )
    small = lax.psum(
        jnp.concatenate([d_router_part.reshape(-1), d_gattn, d_gffn, d_glatent]), BOTH
    )
    count = width * experts
    d_router = lax.dynamic_slice_in_dim(
        small[:count].reshape(width, experts), my_shard * part, part, 0
    )
    gains = small[count:]
    own = lambda v, n: lax.dynamic_slice_in_dim(v, my_shard * n, n, 0)
    part_gattn = own(gains[:width], part)
    part_gffn = own(gains[width : 2 * width], part)
    part_glatent = own(gains[2 * width :], KVR // shards)
    part_query = sum_query.transpose(1, 0, 2).reshape(part, H * (DN + DR)).astype(F32)
    part_expand = (
        sum_expand.transpose(1, 0, 2).reshape(KVR // shards, H * (DN + DV)).astype(F32)
    )
    return (
        output_rows.astype(BF)[None],
        grad_input[None],
        part_query,
        sum_latent.astype(F32),
        part_glatent,
        part_expand,
        sum_out.astype(F32),
        part_gattn,
        part_gffn,
        d_router,
        part_sgate,
        part_sup,
        part_sdown,
        d_egate,
        grad_expert_up,
        d_edown,
    )


def solution(mesh):
    return jax.shard_map(
        body,
        mesh=mesh,
        in_specs=(
            P("expert", "shard", None),
            P("expert", "shard", None),
            P("expert", None),
            P("expert", "shard", None),
            P("shard", None),
            P("shard", None),
            P("shard"),
            P("shard", None),
            P("shard", None),
            P("shard"),
            P("shard"),
            P("shard", None),
            P("shard", None),
            P("shard", None),
            P("shard", None),
            P("expert", None, "shard"),
            P("expert", None, "shard"),
            P("expert", "shard", None),
        ),
        out_specs=(
            P("expert", "shard", None),
            P("expert", "shard", None),
            P("shard", None),
            P("shard", None),
            P("shard"),
            P("shard", None),
            P("shard", None),
            P("shard"),
            P("shard"),
            P("shard", None),
            P("shard", None),
            P("shard", None),
            P("shard", None),
            P("expert", None, "shard"),
            P("expert", None, "shard"),
            P("expert", "shard", None),
        ),
        check_vma=False,
    )
```

time: 3950 us -> 1470 us (0.37)
  waiting for transfers between devices: 2670 us -> 694 us
  blocking collectives: 583 us -> 198 us
  matrix products: 356 us -> 205 us
  Pallas kernels: 0 us -> 148 us
  local copies, waits for them, and re-layouts: 197 us -> 87.3 us
    all_to_all x8 -> x10, waiting for transfers between devices: 1210 us -> 172 us  [exchange(): return lax.all_to_all(values, axis, split_axis=0, concat_axis=0, tiled=True)]
    all_gather x7 -> x5, waiting for transfers between devices: 664 us -> 0.02 us  [the longest x1 0.02 us: body(): g_all = lax.all_gather(cotangent[0], BOTH, axis=0, tiled=False)]
    all_to_all x7 -> x2, blocking collectives: 518 us -> 51.1 us  [exchange(): return lax.all_to_all(values, axis, split_axis=0, concat_axis=0, tiled=True)]
    psum x1 -> x2, waiting for transfers between devices: 797 us -> 361 us  [the longest x1 227 us: body(): lax.psum((rows_query, rows_latent, rows_expand, d_out), 'expert')]
    reduce_scatter x2, waiting for transfers between devices: 0.01 us -> 160 us  [the longest x1 87.8 us: body(): lax.psum_scatter(dn2_part, BOTH, scatter_dimension=0, tiled=False)]
    dot_general x42 -> x21, matrix products: 356 us -> 205 us  [the longest x5 23 us: mm(): return jnp.dot(a, b, preferred_element_type=F32)]
    pallas_call x0 -> x6, Pallas kernels: none -> 148 us  [the longest x2 58.1 us: place_rows(): pl.pallas_call(place_kernel, grid=(devices,), in_specs=[pl.BlockSpec((1,...]
    all_gather x5 -> x4, blocking collectives: 34.5 us -> 147 us  [the longest x1 56.2 us: body(): lax.all_gather(jnp.concatenate([g_attn, g_ffn, g_latent]), 'shard', axis=...]
  transfers between devices with their start and end apart: 18 -> 19, of which waited for: 14 -> 12; matrix products, arithmetic and copies ran while one was open for 10% -> 16% of each run, Pallas kernels for 0% -> 6%
where the time goes in v1:
time: 1470 us; the launch traced here: 1450 us
  waiting for transfers between devices  694 us (47%)
  matrix products  205 us (14%)
  blocking collectives  198 us (13%)
  Pallas kernels  148 us (10%)
  local copies, waits for them, and re-layouts  87.3 us (6%)
  other arithmetic  61.5 us (4%)
  starting transfers between devices  43.3 us (3%)
  between operations  15.2 us (1%)
    psum x1, waiting for transfers between devices, body(): lax.psum((rows_query, rows_latent, rows_expand, d_out), 'expert')  227 us
    all_to_all x10, waiting for transfers between devices, exchange(): return lax.all_to_all(values, axis, split_axis=0, concat_axis=0, tiled=True)  172 us
    psum x1, waiting for transfers between devices, body(): lax.psum(jnp.concatenate([d_router_part.reshape(-1), d_gattn, d_gffn, d_g...  134 us
    reduce_scatter x1, waiting for transfers between devices, body(): lax.psum_scatter(dn2_part, BOTH, scatter_dimension=0, tiled=False)  87.8 us
    reduce_scatter x1, waiting for transfers between devices, body(): lax.psum_scatter(out_part, BOTH, scatter_dimension=0, tiled=False)  72.1 us
    pallas_call x2, Pallas kernels, place_rows(): pl.pallas_call(place_kernel, grid=(devices,), in_specs=[pl.BlockSpec((1,...  58.1 us
    all_gather x1, blocking collectives, body(): lax.all_gather(jnp.concatenate([g_attn, g_ffn, g_latent]), 'shard', axis=...  56.2 us
    pallas_call x2, Pallas kernels, pick_rows(): pl.pallas_call(pick_kernel, grid=(devices,), in_specs=[pl.BlockSpec((1, s...  53.2 us
  transfers between devices with their start and end apart: 19, of which 12 were waited for; matrix products, arithmetic and copies ran while one was open for 16% of the time, Pallas kernels for 6%

profile of v1, /device:TPU:0, one launch (start us, length us, event | category | flops | bytes accessed | tf_op | source)
XLA Modules:
  0.0 1452.6 jit_solution(11455467957117526761)
XLA Ops:
  15.8 4.7 copy.180
  20.5 34.3 %all-to-all-done = bf16[4,128,2048]{2,1,0:T(8,128)(2,1)} async-done(((bf16[4,128,2048]{2,1,0:T(8,128)(2,1)}), bf16[4,128,2048]{2,1,0:T(8,128)(2,1)}, u32[]{:S(2)}, u32[]{:S(2)}) %all-to-all-start) | async-done | bytes 2097184 | tf_op jit(solution)/shard_map/all_to_all | solution.py:80
  54.8 4.8 all-to-all-start.1
  59.7 56.2 %all-gather.2 = bf16[4,1,1152]{2,1,0:T(2,128)(2,1)S(1)} all-gather(bf16[1,1,1152]{2,1,0:T(2,128)(2,1)S(1)} %reshape.387), channel_id=2, replica_groups=mesh['expert'=8,'shard'=4] {'shard'}, dimensions={0}, use_global_device_ids=true | all-gather | bytes 11520 | tf_op jit(solution)/shard_map/all_gather | solution.py:344
  129.0 6.2 copy.181
  142.5 11.8 all-to-all-done.2
  154.4 12.6 attention_forward.1
  175.2 25.7 %all-to-all-done.3 = bf16[4,128,2048]{2,1,0:T(8,128)(2,1)} async-done(((bf16[4,128,2048]{2,1,0:T(8,128)(2,1)}), bf16[4,128,2048]{2,1,0:T(8,128)(2,1)}, u32[]{:S(2)}, u32[]{:S(2)}) %all-to-all-start.3) | async-done | bytes 2097184 | tf_op jit(solution)/shard_map/all_to_all | solution.py:80
  222.3 45.3 %all_gather.38 = s32[32,128,6]{1,2,0:T(8,128)S(1)} all-gather(s32[1,128,6]{1,2,0:T(8,128)S(1)} %copy.190), channel_id=1, replica_groups=mesh['expert'=8,'shard'=4] {'expert','shard'}, dimensions={0}, use_global_device_ids=true | all-gather | bytes 101376 | tf_op jit(solution)/shard_map/all_gather | solution.py:373
  271.6 6.3 all_gather.39
  281.7 39.0 %all_gather.40 = f32[32,128,6]{1,2,0:T(8,128)S(1)} all-gather(f32[1,128,6]{1,2,0:T(8,128)S(1)} %fusion.43), channel_id=1, replica_groups=mesh['expert'=8,'shard'=4] {'expert','shard'}, dimensions={0}, use_global_device_ids=true | all-gather | bytes 101376 | tf_op jit(solution)/shard_map/all_gather | solution.py:403
  322.3 26.6 %pick_rows.3 = bf16[4,1024,2048]{2,1,0:T(8,128)(2,1)} custom-call(bf16[32,128,128]{2,1,0:T(8,128)(2,1)} %convert_element_type.268.pick_ref, bf16[32,128,2048]{2,1,0:T(8,128)(2,1)} %all-gather.13.cloned.1.call-done.x_ref), custom_call_target="tpu_custom_call" | custom-call | tf_op jit(solution)/shard_map/pick_rows/pallas_call | solution.py:260
  348.9 13.0 fusion.55
  361.9 13.1 fusion.54
  375.0 12.8 multiply_convert_fusion.4
  390.2 26.6 %pick_rows.2 = bf16[4,1024,2048]{2,1,0:T(8,128)(2,1)} custom-call(bf16[32,128,128]{2,1,0:T(8,128)(2,1)} %convert_element_type.268.pick_ref, bf16[32,128,2048]{2,1,0:T(8,128)(2,1)} %all-gather.11.cloned.1.call-done.x_ref), custom_call_target="tpu_custom_call" | custom-call | tf_op jit(solution)/shard_map/pick_rows/pallas_call | solution.py:260
  416.8 13.2 fusion.53
  430.0 18.4 %multiply_convert_fusion.1 = (bf16[4,1024,352]{1,2,0:T(8,128)(2,1)}, f32[4,1024]{1,0:T(4,128)S(1)}, bf16[4,1024,352]{1,2,0:T(8,128)(2,1)}, bf16[4,1024,352]{1,2,0:T(8,128)(2,1)}) fusion(f32[4,1024,352]{1,2,0:T(8,128)} %fusion.53, f32[4,1024,352]{1,2,0:T(8,128)} %fusion.55, f32[4,1024]{1,0:T(4,128)S(1)} %mul.418, bf16[4,1024,2048]{2,1,0:T(8,128)(2,1)} %pick_rows.2, ...), kind=kOutput, calls=%fused_computation.8 | convolution fusion | flops 5935853568 | bytes 42762240 | tf_op jit(solution)/shard_map/jmd,jdf->jmf/dot_general | solution.py:416
  448.4 17.3 %fusion.56 = f32[4,1024,2048]{2,1,0:T(8,128)} fusion(bf16[4,1024,352]{1,2,0:T(8,128)(2,1)} %get-tuple-element.128, bf16[4,2048,352]{1,2,0:T(8,128)(2,1)S(1)} %bitcast.173), kind=kOutput, calls=%fused_computation.145 | convolution fusion | flops 5905580032 | bytes 42205184 | tf_op jit(solution)/shard_map/jmf,jdf->jmd/dot_general | solution.py:433
  467.9 20.9 %add_convert_fusion.rows_ref = bf16[4,1024,2048]{2,1,0:T(8,128)(2,1)} fusion(f32[4,1024,2048]{2,1,0:T(8,128)} %fusion.56, bf16[4,1024,352]{1,2,0:T(8,128)(2,1)S(1)} %copy-done.14, bf16[4,2048,352]{1,2,0:T(8,128)(2,1)} %param.34), kind=kOutput, calls=%fused_computation | convolution fusion | flops 5922357248 | bytes 58982400 | tf_op jit(solution)/shard_map/jmf,jdf->jmd/dot_general | solution.py:434
  488.8 29.1 %place_rows.3 = bf16[32,128,2048]{2,1,0:T(8,128)(2,1)} custom-call(bf16[32,128,128]{2,1,0:T(8,128)(2,1)} %convert_element_type.268.pick_ref, bf16[4,1024,2048]{2,1,0:T(8,128)(2,1)} %add_convert_fusion.rows_ref, bf16[32,128,176]{2,1,0:T(8,128)(2,1)} %pad_maximum_fusion.left_ref, bf16[176,2048]{1,0:T(8,128)(2,1)} %bitcast.185), custom_call_target="tpu_custom_call" | custom-call | tf_op jit(solution)/shard_map/place_rows/pallas_call | solution.py:285
  518.0 9.8 convolution_convert_fusion.4
  528.0 9.3 convolution_convert_fusion.3
  537.3 22.2 %all_to_all.64 = bf16[4,176,512]{2,1,0:T(8,128)(2,1)} all-to-all(bf16[4,176,512]{2,1,0:T(8,128)(2,1)S(1)} %bitcast.183), channel_id=1, replica_groups=mesh['expert'=8,'shard'=4] {'shard'}, dimensions={0} | all-to-all | bytes 1441792 | tf_op jit(solution)/shard_map/all_to_all | solution.py:80
  561.3 15.5 %convolution_convert_fusion.rows_ref = bf16[4,1024,2048]{2,1,0:T(8,128)(2,1)} fusion(bf16[4,1024,352]{1,2,0:T(8,128)(2,1)} %get-tuple-element.131, bf16[4,352,2048]{2,1,0:T(8,128)(2,1)} %param.35), kind=kOutput, calls=%fused_computation.3 | convolution fusion | flops 5913968640 | bytes 25427968 | tf_op jit(solution)/shard_map/jmf,jfd->jmd/dot_general | solution.py:440
  576.8 29.0 %place_rows.2 = bf16[32,128,2048]{2,1,0:T(8,128)(2,1)} custom-call(bf16[32,128,128]{2,1,0:T(8,128)(2,1)} %convert_element_type.268.pick_ref, bf16[4,1024,2048]{2,1,0:T(8,128)(2,1)} %convolution_convert_fusion.rows_ref, bf16[32,128,88]{2,1,0:T(8,128)(2,1)} %bitcast.175, bf16[88,2048]{1,0:T(8,128)(2,1)} %copy-done.17), custom_call_target="tpu_custom_call" | custom-call | tf_op jit(solution)/shard_map/place_rows/pallas_call | solution.py:285
  610.1 7.0 all-to-all-done.5
  617.8 87.8 %reduce-scatter.5.cloned.1.call-done = bf16[1,128,2048]{2,1,0:T(8,128)(2,1)} async-done(((bf16[32,128,2048]{2,1,0:T(8,128)(2,1)}), bf16[1,128,2048]{2,1,0:T(8,128)(2,1)}) %reduce-scatter.5.cloned.1.call-update) | async-done | bytes 524304 | tf_op jit(solution)/shard_map/reduce_scatter | solution.py:439
  707.8 28.9 %all_to_all.65 = bf16[4,128,2048]{2,1,0:T(8,128)(2,1)} all-to-all(bf16[4,128,2048]{2,1,0:T(8,128)(2,1)S(1)} %broadcast_in_dim.59), channel_id=1, replica_groups=mesh['expert'=8,'shard'=4] {'shard'}, dimensions={0} | all-to-all | bytes 4194304 | tf_op jit(solution)/shard_map/all_to_all | solution.py:80
  736.7 24.0 %attention_backward.1 = (f32[512,2048]{1,0:T(8,128)}, f32[512,576]{1,0:T(8,128)}, bf16[4,4,512,192]{3,2,1,0:T(8,128)(2,1)}, bf16[4,4,128,256]{3,2,1,0:T(8,128)(2,1)}, bf16[512,2048]{1,0:T(8,128)(2,1)}) custom-call(bf16[512,2048]{1,0:T(8,128)(2,1)} %bitcast.171, bf16[512,2048]{1,0:T(8,128)(2,1)} %wo_ref.1, bf16[512,512]{1,0:T(8,128)(2,1)} %get-tuple-element.25.o_ref, ...), custom_call_target="tpu_custom_call" | custom-call | tf_op jit(solution)/shard_map/attention_backward/pallas_call | solution.py:214
  770.7 4.9 add_convert_fusion.1
  788.8 21.1 %all-to-all-done.7 = bf16[4,128,2048]{2,1,0:T(8,128)(2,1)} async-done(((bf16[4,128,2048]{2,1,0:T(8,128)(2,1)}), bf16[4,128,2048]{2,1,0:T(8,128)(2,1)}, u32[]{:S(2)}, u32[]{:S(2)}) %all-to-all-start.7) | async-done | bytes 2097184 | tf_op jit(solution)/shard_map/all_to_all | solution.py:80
  814.4 6.0 copy.204
  820.4 22.5 %all-to-all-done.9 = bf16[4,512,576]{1,2,0:T(8,128)(2,1)} async-done(((bf16[4,512,576]{1,2,0:T(8,128)(2,1)}), bf16[4,512,576]{1,2,0:T(8,128)(2,1)}, u32[]{:S(2)}, u32[]{:S(2)}) %all-to-all-start.9) | async-done | bytes 2359328 | tf_op jit(solution)/shard_map/all_to_all | solution.py:80
  857.0 45.1 %all-to-all-done.8 = bf16[16,512,192]{1,2,0:T(8,128)(2,1)} async-done(((bf16[16,512,192]{1,2,0:T(8,128)(2,1)}), bf16[16,512,192]{1,2,0:T(8,128)(2,1)}, u32[]{:S(2)}, u32[]{:S(2)}) %all-to-all-start.8) | async-done | bytes 3145760 | tf_op jit(solution)/shard_map/all_to_all | solution.py:80
  902.2 15.6 %fusion.57 = f32[4,352,2048]{2,1,0:T(8,128)} fusion(bf16[4,1024,352]{1,2,0:T(8,128)(2,1)} %get-tuple-element.131, bf16[4,1024,2048]{2,1,0:T(8,128)(2,1)} %pick_rows.3), kind=kOutput, calls=%fused_computation.146 | convolution fusion | flops 5905580032 | bytes 31195136 | tf_op jit(solution)/shard_map/jmf,jmd->jfd/dot_general | solution.py:451
  917.8 15.5 %fusion.58 = f32[4,2048,352]{1,2,0:T(8,128)} fusion(bf16[4,1024,352]{1,2,0:T(8,128)(2,1)} %get-tuple-element.128, bf16[4,1024,2048]{2,1,0:T(8,128)(2,1)} %pick_rows.2), kind=kOutput, calls=%fused_computation.147 | convolution fusion | flops 5905580032 | bytes 31195136 | tf_op jit(solution)/shard_map/jmd,jmf->jdf/dot_general | solution.py:452
  933.3 10.9 fusion.59
  944.2 5.1 convert_element_type.305
  949.3 8.6 convert_bitcast_fusion
  957.9 8.5 fusion.50
  969.6 6.5 copy.214
  976.1 6.1 copy.209
  982.2 6.3 copy.213
  988.6 72.1 %reduce-scatter.3.cloned.1.call-done = bf16[1,128,2048]{2,1,0:T(8,128)(2,1)} async-done(((bf16[32,128,2048]{2,1,0:T(8,128)(2,1)}), bf16[1,128,2048]{2,1,0:T(8,128)(2,1)}) %reduce-scatter.3.cloned.1.call-update) | async-done | bytes 524304 | tf_op jit(solution)/shard_map/reduce_scatter | solution.py:446
  1064.5 134.2 %all-reduce.4.cloned.1.call-done = f32[70144]{0:T(1024)} async-done(((f32[70144]{0:T(1024)}), f32[70144]{0:T(1024)}) %all-reduce.4.cloned.1.call-update) | async-done | bytes 280592 | tf_op jit(solution)/shard_map/psum | solution.py:506
  1204.0 227.1 %all-reduce.6.cloned.1.call-done = (bf16[512,3072]{0,1:T(8,128)(2,1)}, bf16[512,576]{0,1:T(8,128)(2,1)}, bf16[128,4096]{1,0:T(8,128)(2,1)}, bf16[512,2048]{1,0:T(8,128)(2,1)}) async-done(((bf16[512,3072]{0,1:T(8,128)(2,1)}, bf16[512,576]{0,1:T(8,128)(2,1)}, bf16[128,4096]{1,0:T(8,128)(2,1)}, bf16[512,2048]{1,0:T(8,128)(2,1)}), (bf16[512,3072]{0,1:T(8,128)(2,1)}, bf16[512,576]{0,1:T(8,128)(2,1)}, ...) | async-done | bytes 6881296 | tf_op jit(solution)/shard_map/psum | solution.py:503
  1436.1 5.4 copy.211
  (266 shorter events, 144.4 us)
Async XLA Ops:
  7.2 270.7 %copy-start = (bf16[704,2048]{1,0:T(8,128)(2,1)S(1)}, bf16[704,2048]{1,0:T(8,128)(2,1)}, u32[]{:S(2)}) copy-start(bf16[704,2048]{1,0:T(8,128)(2,1)} %param.32) | copy-start | bytes 8650756
  7.2 128.0 %all-gather.9.cloned.1.call-start = ((), (), s32[]{:S(2)}) async-start(), calls=%async_computation.14 | async-start | bytes 2949120 | tf_op jit(solution)/shard_map/all_gather | solution.py:343
  7.9 314.4 %all-gather.13.cloned.1.call-start = ((), (), s32[]{:S(2)}) async-start(), calls=%async_computation.17 | async-start | bytes 17301504 | tf_op jit(solution)/shard_map/all_gather | solution.py:351
  11.3 43.5 %all-to-all-start = ((bf16[4,128,2048]{2,1,0:T(8,128)(2,1)}), bf16[4,128,2048]{2,1,0:T(8,128)(2,1)}, u32[]{:S(2)}, u32[]{:S(2)}) async-start(bf16[4,128,2048]{2,1,0:T(8,128)(2,1)} %broadcast_in_dim.51), calls=%async_computation | async-start | bytes 4194304 | tf_op jit(solution)/shard_map/all_to_all | solution.py:80
  54.8 61.1 %copy-start.43 = (s32[1,512]{1,0:T(1,128)S(1)}, s32[1,512]{1,0:T(1,128)}, u32[]{:S(2)}) copy-start(s32[1,512]{1,0:T(1,128)} %segr_ref.3) | copy-start | bytes 6148
  54.8 69.9 %all-to-all-start.1 = ((bf16[16,512,192]{1,2,0:T(8,128)(2,1)}), bf16[16,512,192]{1,2,0:T(8,128)(2,1)}, u32[]{:S(2)}, u32[]{:S(2)}) async-start(bf16[16,512,192]{1,2,0:T(8,128)(2,1)} %bitcast.169), calls=%async_computation.1 | async-start | bytes 6291456 | tf_op jit(solution)/shard_map/all_to_all | solution.py:80
  124.7 29.6 %all-to-all-start.2 = ((bf16[16,128,256]{2,1,0:T(8,128)(2,1)}), bf16[16,128,256]{2,1,0:T(8,128)(2,1)}, u32[]{:S(2)}, u32[]{:S(2)}) async-start(bf16[16,128,256]{2,1,0:T(8,128)(2,1)} %bitcast.177), calls=%async_computation.2 | async-start | bytes 2097152 | tf_op jit(solution)/shard_map/all_to_all | solution.py:80
  139.5 27.4 %copy-start.40 = (f32[512]{0:T(512)}, f32[512]{0:T(512)S(1)}, u32[]{:S(2)}) copy-start(f32[512]{0:T(512)S(1)} %add_rsqrt_fusion) | copy-start | bytes 6148
  170.6 32.4 %copy-start.3 = (bf16[1,128,2048]{2,1,0:T(8,128)(2,1)S(1)}, bf16[1,128,2048]{2,1,0:T(8,128)(2,1)}, u32[]{:S(2)}) copy-start(bf16[1,128,2048]{2,1,0:T(8,128)(2,1)} %param.18) | copy-start | bytes 1572868
  170.6 30.3 %all-to-all-start.3 = ((bf16[4,128,2048]{2,1,0:T(8,128)(2,1)}), bf16[4,128,2048]{2,1,0:T(8,128)(2,1)}, u32[]{:S(2)}, u32[]{:S(2)}) async-start(bf16[4,128,2048]{2,1,0:T(8,128)(2,1)} %bitcast.188), calls=%async_computation.3 | async-start | bytes 4194304 | tf_op jit(solution)/shard_map/all_to_all | solution.py:80
  175.2 186.7 %all-gather.11.cloned.1.call-start = ((), (), s32[]{:S(2)}) async-start(), calls=%async_computation.15 | async-start | bytes 17301504 | tf_op jit(solution)/shard_map/all_gather | solution.py:398
  175.2 104.0 %copy-start.25 = (f32[1,4,4,128]{3,1,2,0:T(4,128)}, f32[1,4,4,128]{3,1,2,0:T(4,128)S(1)}, u32[]{:S(2)}) copy-start(f32[1,4,4,128]{3,1,2,0:T(4,128)S(1)} %copy.225) | copy-start | bytes 24580
  204.8 74.4 %copy-start.44 = (f32[128]{0:T(128)}, f32[128]{0:T(128)S(1)}, u32[]{:S(2)}) copy-start(f32[128]{0:T(128)S(1)} %add_rsqrt_fusion.2) | copy-start | bytes 1540
  216.2 55.4 %copy-start.37 = (bf16[512,32]{0,1:T(8,128)(2,1)S(1)}, bf16[512,32]{0,1:T(8,128)(2,1)}, u32[]{:S(2)}) copy-start(bf16[512,32]{0,1:T(8,128)(2,1)} %param.29) | copy-start | bytes 98308
  217.1 60.8 %all-to-all-start.4 = ((bf16[4,512,176]{1,2,0:T(8,128)(2,1)}), bf16[4,512,176]{1,2,0:T(8,128)(2,1)}, u32[]{:S(2)}, u32[]{:S(2)}) async-start(bf16[4,512,176]{1,2,0:T(8,128)(2,1)} %maximum_bitcast_fusion), calls=%async_computation.4 | async-start | bytes 1441792 | tf_op jit(solution)/shard_map/all_to_all | solution.py:80
  221.3 484.3 %reduce-scatter.5.cloned.1.call-start = ((), (), s32[]{:S(2)}) async-start(), calls=%async_computation.18 | async-start | bytes 17301504 | tf_op jit(solution)/shard_map/reduce_scatter | solution.py:439
  221.4 59.7 %copy-start.33 = (s32[1,128,6]{1,2,0:T(8,128)}, s32[1,128,6]{1,2,0:T(8,128)S(1)}, u32[]{:S(2)}) copy-start(s32[1,128,6]{1,2,0:T(8,128)S(1)} %copy.235) | copy-start | bytes 9220
  221.5 50.0 %copy-start.23 = (s32[1,128,6]{2,1,0:T(8,128)}, s32[1,128,6]{2,1,0:T(8,128)S(1)}, u32[]{:S(2)}) copy-start(s32[1,128,6]{2,1,0:T(8,128)S(1)} %copy.188) | copy-start | bytes 9220
  222.0 49.5 %copy-start.31 = (s32[768]{0:T(1024)}, s32[768]{0:T(1024)S(1)}, u32[]{:S(2)}) copy-start(s32[768]{0:T(1024)S(1)} %convert_element_type.266) | copy-start | bytes 9220
  277.9 71.1 %copy-start.18 = (bf16[2048,32]{0,1:T(8,128)(2,1)}, bf16[2048,32]{0,1:T(8,128)(2,1)S(1)}, u32[]{:S(2)}) copy-start(bf16[2048,32]{0,1:T(8,128)(2,1)S(1)} %all_gather.39) | copy-start | bytes 393220
  277.9 97.1 %copy-start.17 = (bf16[88,2048]{1,0:T(8,128)(2,1)}, bf16[88,2048]{1,0:T(8,128)(2,1)S(1)}, u32[]{:S(2)}) copy-start(bf16[88,2048]{1,0:T(8,128)(2,1)S(1)} %constant_dynamic-slice_fusion.1.right_ref) | copy-start | bytes 1081348
  279.2 82.7 %copy-start.15 = (bf16[4,22,8,512]{3,2,0,1:T(8,128)(2,1)}, bf16[4,22,8,512]{3,2,0,1:T(8,128)(2,1)S(1)}, u32[]{:S(2)}) copy-start(bf16[4,22,8,512]{3,2,0,1:T(8,128)(2,1)S(1)} %copy.222) | copy-start | bytes 2162692
  281.2 67.7 %copy-start.35 = (f32[128,6]{0,1:T(8,128)}, f32[128,6]{0,1:T(8,128)S(1)}, u32[]{:S(2)}) copy-start(f32[128,6]{0,1:T(8,128)S(1)} %get-tuple-element.121) | copy-start | bytes 9220
  281.2 67.7 %copy-start.48 = (f32[128]{0:T(128)}, f32[128]{0:T(128)S(1)}, u32[]{:S(2)}) copy-start(f32[128]{0:T(128)S(1)} %get-tuple-element.120) | copy-start | bytes 1540
  416.8 31.6 %slice-start.4 = ((s8[5767168]{0:T(1024)(128)(4,1)}), s8[1572864]{0:T(1024)(128)(4,1)S(1)}, s32[]{:S(2)}) async-start(s8[5767168]{0:T(1024)(128)(4,1)} %bitcast.172), calls=%async_computation.27 | async-start | bytes 3145728
  518.0 426.2 %all-gather.15.cloned.1.call-start = ((), (), s32[]{:S(2)}) async-start(), calls=%async_computation.20 | async-start | bytes 3244032 | tf_op jit(solution)/shard_map/all_gather | solution.py:477
  527.9 421.4 %all-gather.17.cloned.1.call-start = ((), (), s32[]{:S(2)}) async-start(), calls=%async_computation.21 | async-start | bytes 6488064 | tf_op jit(solution)/shard_map/all_gather | solution.py:472
  559.5 501.2 %reduce-scatter.3.cloned.1.call-start = ((), (), s32[]{:S(2)}) async-start(), calls=%async_computation.16 | async-start | bytes 17301504 | tf_op jit(solution)/shard_map/reduce_scatter | solution.py:446
  605.8 99.8 %copy-start.2 = (f32[128,2048]{1,0:T(8,128)S(1)}, f32[128,2048]{1,0:T(8,128)}, u32[]{:S(2)}) copy-start(f32[128,2048]{1,0:T(8,128)} %get-tuple-element.127) | copy-start | bytes 3145732
  605.8 99.8 %copy-start.19 = (bf16[2048,32]{0,1:T(8,128)(2,1)S(1)}, bf16[2048,32]{0,1:T(8,128)(2,1)}, u32[]{:S(2)}) copy-start(bf16[2048,32]{0,1:T(8,128)(2,1)} %copy-done.18) | copy-start | bytes 393220
  605.8 99.8 %copy-start.26 = (f32[1,4,4,128]{3,1,2,0:T(4,128)S(1)}, f32[1,4,4,128]{3,1,2,0:T(4,128)}, u32[]{:S(2)}) copy-start(f32[1,4,4,128]{3,1,2,0:T(4,128)} %copy-done.25) | copy-start | bytes 24580
  605.8 99.8 %copy-start.45 = (f32[128]{0:T(128)S(1)}, f32[128]{0:T(128)}, u32[]{:S(2)}) copy-start(f32[128]{0:T(128)} %copy-done.44) | copy-start | bytes 1540
  606.4 100.8 %copy-start.13 = (bf16[1,128,2048]{2,1,0:T(8,128)(2,1)S(1)}, bf16[1,128,2048]{2,1,0:T(8,128)(2,1)}, u32[]{:S(2)}) copy-start(bf16[1,128,2048]{2,1,0:T(8,128)(2,1)} %param.19) | copy-start | bytes 1572868
  607.4 9.7 all-to-all-start.5
  707.2 29.5 %copy-start.9 = (f32[128,2048]{1,0:T(8,128)}, f32[128,2048]{1,0:T(8,128)S(1)}, u32[]{:S(2)}) copy-start(f32[128,2048]{1,0:T(8,128)S(1)} %get-tuple-element.148) | copy-start | bytes 3145732
  736.7 28.5 %copy-start.6 = (f32[512,576]{1,0:T(8,128)S(1)}, f32[512,576]{1,0:T(8,128)}, u32[]{:S(2)}) copy-start(f32[512,576]{1,0:T(8,128)} %copy-done.5) | copy-start | bytes 3538948
  736.7 28.5 %copy-start.39 = (f32[512]{0:T(512)S(1)}, f32[512]{0:T(512)}, u32[]{:S(2)}) copy-start(f32[512]{0:T(512)} %copy-done.38) | copy-start | bytes 6148
  736.7 28.5 %copy-start.41 = (f32[512]{0:T(512)S(1)}, f32[512]{0:T(512)}, u32[]{:S(2)}) copy-start(f32[512]{0:T(512)} %copy-done.40) | copy-start | bytes 6148
  760.8 18.9 %all-to-all-start.10 = ((bf16[16,128,256]{2,1,0:T(8,128)(2,1)}), bf16[16,128,256]{2,1,0:T(8,128)(2,1)}, u32[]{:S(2)}, u32[]{:S(2)}) async-start(bf16[16,128,256]{2,1,0:T(8,128)(2,1)} %bitcast.190), calls=%async_computation.12 | async-start | bytes 2097152 | tf_op jit(solution)/shard_map/all_to_all | solution.py:80
  779.7 30.2 %all-to-all-start.7 = ((bf16[4,128,2048]{2,1,0:T(8,128)(2,1)}), bf16[4,128,2048]{2,1,0:T(8,128)(2,1)}, u32[]{:S(2)}, u32[]{:S(2)}) async-start(bf16[4,128,2048]{2,1,0:T(8,128)(2,1)} %bitcast.187), calls=%async_computation.9 | async-start | bytes 4194304 | tf_op jit(solution)/shard_map/all_to_all | solution.py:80
  809.9 33.0 %all-to-all-start.9 = ((bf16[4,512,576]{1,2,0:T(8,128)(2,1)}), bf16[4,512,576]{1,2,0:T(8,128)(2,1)}, u32[]{:S(2)}, u32[]{:S(2)}) async-start(bf16[4,512,576]{1,2,0:T(8,128)(2,1)} %bitcast.170), calls=%async_computation.11 | async-start | bytes 4718592 | tf_op jit(solution)/shard_map/all_to_all | solution.py:80
  842.9 59.2 %all-to-all-start.8 = ((bf16[16,512,192]{1,2,0:T(8,128)(2,1)}), bf16[16,512,192]{1,2,0:T(8,128)(2,1)}, u32[]{:S(2)}, u32[]{:S(2)}) async-start(bf16[16,512,192]{1,2,0:T(8,128)(2,1)} %copy.204), calls=%async_computation.10 | async-start | bytes 6291456 | tf_op jit(solution)/shard_map/all_to_all | solution.py:80
  847.6 351.1 %all-reduce.4.cloned.1.call-start = ((), (), s32[]{:S(2)}) async-start(), calls=%async_computation.19 | async-start | bytes 565248 | tf_op jit(solution)/shard_map/psum | solution.py:506
  851.6 579.5 %all-reduce.6.cloned.1.call-start = ((), (), s32[]{:S(2)}) async-start(), calls=%async_computation.22 | async-start | bytes 13762560 | tf_op jit(solution)/shard_map/psum | solution.py:503
  902.1 31.1 %slice-start = ((s8[16777216]{0:T(1024)(128)(4,1)}), s8[4194304]{0:T(1024)(128)(4,1)S(1)}, s32[]{:S(2)}) async-start(s8[16777216]{0:T(1024)(128)(4,1)} %bitcast.165), calls=%async_computation.23 | async-start | bytes 8388608
  902.1 31.1 %slice-start.1 = ((s8[16777216]{0:T(1024)(128)(4,1)}), s8[4194304]{0:T(1024)(128)(4,1)S(1)}, s32[]{:S(2)}) async-start(s8[16777216]{0:T(1024)(128)(4,1)} %bitcast.165), calls=%async_computation.24 | async-start | bytes 8388608
  902.2 31.1 %slice-start.2 = ((s8[16777216]{0:T(1024)(128)(4,1)}), s8[4194304]{0:T(1024)(128)(4,1)S(1)}, s32[]{:S(2)}) async-start(s8[16777216]{0:T(1024)(128)(4,1)} %bitcast.165), calls=%async_computation.25 | async-start | bytes 8388608
  982.2 78.5 %copy-start.8 = (f32[128,2048]{1,0:T(8,128)S(1)}, f32[128,2048]{1,0:T(8,128)}, u32[]{:S(2)}) copy-start(f32[128,2048]{1,0:T(8,128)} %copy-done.7) | copy-start | bytes 3145732
  (34 other events, 288.1 us)
Sparse Core Ops, SparseCore 0:
  9.6 39.4 all-gather.8
  52.0 143.3 all-gather.12
  206.0 117.6 all-gather.10
  518.1 187.4 reduce-scatter.4
  707.6 60.1 all-gather.14
  769.9 90.9 all-gather.16
  863.2 197.4 reduce-scatter.2
  1066.0 132.6 all-reduce.3
  1203.8 227.2 all-reduce.5
